TPU v7x, 256 devices: a whole 4x4x8 slice. The times are simulated.
256 devices in a mesh: fsdp: 32 (over z_hi, x, core), dp: 8 (over y, z_lo).
Axes of the slice: x: 4, y: 4, z: 8 (z_hi: 4, z_lo: 2; z = z_hi * 2 + z_lo), core: 2. Of those that a mesh axis runs over, the one named last changes fastest.
Arguments:
- activations: bfloat16 [65536, 4096], P(('fsdp', 'dp')), may hold values from -6 to 6
- cotangents: bfloat16 [2, 65536, 4096], P(None, ('fsdp', 'dp')), may hold values from -6 to 6
- weights: bfloat16 [2, 4096, 4096], P(None, 'fsdp'), may hold values from -4 to 4
- projectors: bfloat16 [2, 4096, 512], P(None, 'fsdp'), may hold values from -0.09375 to 0.09375
- first_moment: float32 [2, 4096, 512], P(None, 'fsdp'), may hold values from -3 to 3
- second_moment: float32 [2, 4096, 512], P(None, 'fsdp'), may hold values from 0.25 to 4
- matrix_settings: int32 [2, 2], replicated, may hold values from 0 to 512, as said below
Outputs:
- new_weights: bfloat16 [2, 4096, 4096], P(None, 'fsdp')
- new_first: float32 [2, 4096, 512], P(None, 'fsdp')
- new_second: float32 [2, 4096, 512], P(None, 'fsdp')
Inputs may be any that keep to these rules, and one draw needn't show every extreme that they name: `matrix_settings`: column 0 is a rank from 128 to 512, some matrix has rank exactly 512; column 1 is 0 (the projector acts on the activations) or 1 (on the cotangents), and both values occur.
All inputs are finite; a program needn't handle non-finite values.
Results may differ from a plain program's by a relative error of at most 0.0045.
Values may be sent and summed in bfloat16 or wider, within the bound.
No kernel may reach another device: no remote copies, remote signals or barrier semaphores. Data moves between devices by JAX's collectives and lax.ppermute only.
A program may use at most 128 MiB of HBM per device.

v0:
```python
import math

import jax
import jax.numpy as jnp
from jax import lax
from jax.sharding import PartitionSpec as P

BETA_ONE = 0.9
BETA_TWO = 0.95
EPSILON = 1e-08


def on_device(
    activations, cotangents, weights, projectors, first_moment, second_moment, matrix_settings
):
    rank_max = projectors.shape[2]
    token_local = activations.shape[0]
    token_total = token_local * lax.axis_size("fsdp") * lax.axis_size("dp")
    grad_scale = 1.0 / math.sqrt(token_total)
    rank_columns = jnp.arange(rank_max)
    weight_list, first_list, second_list = ([], [], [])
    for matrix_index in range(cotangents.shape[0]):
        live_mask = (rank_columns < matrix_settings[matrix_index, 0])[None, :]
        on_inputs = matrix_settings[matrix_index, 1] == 0
        proj_local = jnp.where(live_mask, projectors[matrix_index], jnp.zeros((), jnp.bfloat16))
        grads_out = cotangents[matrix_index]
        projected_side = jnp.where(on_inputs, activations, grads_out)
        other_side = jnp.where(on_inputs, grads_out, activations)
        shard_piece = lax.all_gather(proj_local, "fsdp", axis=0, tiled=True)
        coeff_sum = jnp.dot(projected_side, shard_piece, preferred_element_type=jnp.float32)
        coeff_sum, full_projector = (coeff_sum, shard_piece)
        coeffs = coeff_sum.astype(jnp.bfloat16)
        partial_sums = lax.psum_scatter(
            lax.dot_general(
                other_side, coeffs, (((0,), (0,)), ((), ())), preferred_element_type=jnp.float32
            ),
            "fsdp",
            scatter_dimension=0,
            tiled=True,
        )
        projected = (
            lax.psum(partial_sums.astype(jnp.bfloat16), "dp").astype(jnp.float32) * grad_scale
        )
        moment_one = jnp.where(
            live_mask, BETA_ONE * first_moment[matrix_index] + (1.0 - BETA_ONE) * projected, 0.0
        )
        moment_two = jnp.where(
            live_mask,
            BETA_TWO * second_moment[matrix_index] + (1.0 - BETA_TWO) * projected * projected,
            0.0,
        )
        normalized = jnp.where(
            live_mask, moment_one / (jnp.sqrt(moment_two) + EPSILON), 0.0
        ).astype(jnp.bfloat16)
        update = lax.dot_general(
            normalized, full_projector, (((1,), (1,)), ((), ())), preferred_element_type=jnp.float32
        )
        weight_list.append(
            (weights[matrix_index].astype(jnp.float32) - update).astype(jnp.bfloat16)
        )
        first_list.append(moment_one)
        second_list.append(moment_two)
    return (jnp.stack(weight_list), jnp.stack(first_list), jnp.stack(second_list))


def solution(mesh):
    return jax.shard_map(
        on_device,
        mesh=mesh,
        in_specs=(
            P(("fsdp", "dp"), None),
            P(None, ("fsdp", "dp"), None),
            P(None, "fsdp", None),
            P(None, "fsdp", None),
            P(None, "fsdp", None),
            P(None, "fsdp", None),
            P(),
        ),
        out_specs=(P(None, "fsdp", None), P(None, "fsdp", None), P(None, "fsdp", None)),
        check_vma=False,
    )
```

profile of v0, /device:TPU:2, one launch (start us, length us, event | category | flops | bytes accessed | tf_op | source)
XLA Modules:
  0.0 480.4 jit_solution(6036514137004158276)
XLA Ops:
  7.2 1.5 fusion.56
  8.7 1.3 iota_compare_fusion
  10.0 1.7 bitcast_select_fusion.17
  11.7 0.0 all-gather.3.cloned.1.call-start
  11.8 0.7 all-gather.3.cloned.1.call-update
  12.5 0.0 reduce-scatter.5.cloned.1.call-start
  13.2 61.6 %all-gather.5.cloned.1.call-done = bf16[4096,512]{1,0:T(8,128)(2,1)} async-done(((bf16[128,512]{1,0:T(8,128)(2,1)}), bf16[4096,512]{1,0:T(8,128)(2,1)}) %all-gather.5.cloned.1.call-update) | async-done | bytes 4194320 | tf_op jit(solution)/shard_map/all_gather | solution.py:29
  74.8 9.8 %fusion.4 = f32[4096,512]{1,0:T(8,128)} fusion(bf16[256,4096]{1,0:T(8,128)(2,1)} %param.7, pred[]{:T(512)} %bitcast.11, bf16[2,256,4096]{2,1,0:T(8,128)(2,1)} %param.8, bf16[4096,512]{1,0:T(8,128)(2,1)} %all-gather.5.cloned.1.call-done), kind=kOutput, calls=%fused_computation.9 | convolution fusion | flops 2149711872 | bytes 20972544 | tf_op jit(solution)/shard_map/dot_general | solution.py:34
  84.6 0.0 reduce-scatter.3.cloned.1.call-start
  85.5 50.9 %all-gather.3.cloned.1.call-done = bf16[4096,512]{1,0:T(8,128)(2,1)} async-done(((bf16[128,512]{1,0:T(8,128)(2,1)}), bf16[4096,512]{1,0:T(8,128)(2,1)}) %all-gather.3.cloned.1.call-update) | async-done | bytes 4194320 | tf_op jit(solution)/shard_map/all_gather | solution.py:29
  136.4 9.2 %fusion.6 = f32[4096,512]{1,0:T(8,128)} fusion(bf16[256,4096]{1,0:T(8,128)(2,1)S(1)} %copy-done, pred[]{:T(512)} %bitcast.3, bf16[2,256,4096]{2,1,0:T(8,128)(2,1)} %param.8, bf16[4096,512]{1,0:T(8,128)(2,1)} %all-gather.3.cloned.1.call-done), kind=kOutput, calls=%fused_computation.13 | convolution fusion | flops 2149711872 | bytes 20972544 | tf_op jit(solution)/shard_map/dot_general | solution.py:34
  145.6 0.0 all-reduce.3.cloned.1.call-start
  145.7 113.7 %reduce-scatter.5.cloned.1.call-done = f32[128,512]{1,0:T(8,128)} async-done(((f32[4096,512]{1,0:T(8,128)}), f32[128,512]{1,0:T(8,128)}) %reduce-scatter.5.cloned.1.call-update) | async-done | bytes 262160 | tf_op jit(solution)/shard_map/reduce_scatter | solution.py:33
  259.4 1.6 convert_element_type.52
  261.0 121.5 %reduce-scatter.3.cloned.1.call-done = f32[128,512]{1,0:T(8,128)} async-done(((f32[4096,512]{1,0:T(8,128)}), f32[128,512]{1,0:T(8,128)}) %reduce-scatter.3.cloned.1.call-update) | async-done | bytes 262160 | tf_op jit(solution)/shard_map/reduce_scatter | solution.py:33
  382.5 1.6 convert_element_type.45
  384.2 79.3 %all-reduce.3.cloned.1.call-done = (bf16[128,512]{1,0:T(8,128)(2,1)}, bf16[128,512]{1,0:T(8,128)(2,1)}) async-done(((bf16[128,512]{1,0:T(8,128)(2,1)}, bf16[128,512]{1,0:T(8,128)(2,1)}), (bf16[128,512]{1,0:T(8,128)(2,1)}, bf16[128,512]{1,0:T(8,128)(2,1)})) %all-reduce.3.cloned.1.call-update) | async-done | bytes 262160 | tf_op jit(solution)/shard_map/psum | solution.py:42
  463.5 1.2 fusion.36
  464.8 4.1 fusion.3
  468.9 0.3 copy-done.6
  469.2 1.5 fusion.2
  470.7 1.5 pad_maximum_fusion
  472.2 0.8 pad_maximum_fusion.1
  473.0 0.8 pad_maximum_fusion.2
  (18 shorter events, 0.1 us)
Async XLA Ops:
  7.2 67.7 %all-gather.5.cloned.1.call-start = ((), (), s32[]{:S(2)}) async-start(), calls=%async_computation.4 | async-start | bytes 4325376 | tf_op jit(solution)/shard_map/all_gather | solution.py:29
  11.7 124.7 %all-gather.3.cloned.1.call-start = ((), (), s32[]{:S(2)}) async-start(), calls=%async_computation.2 | async-start | bytes 4325376 | tf_op jit(solution)/shard_map/all_gather | solution.py:29
  12.5 246.9 %reduce-scatter.5.cloned.1.call-start = ((), (), s32[]{:S(2)}) async-start(), calls=%async_computation.5 | async-start | bytes 8650752 | tf_op jit(solution)/shard_map/reduce_scatter | solution.py:33
  84.6 51.8 %copy-start = (bf16[256,4096]{1,0:T(8,128)(2,1)S(1)}, bf16[256,4096]{1,0:T(8,128)(2,1)}, u32[]{:S(2)}) copy-start(bf16[256,4096]{1,0:T(8,128)(2,1)} %param.7) | copy-start | bytes 6291460
  84.6 297.9 %reduce-scatter.3.cloned.1.call-start = ((), (), s32[]{:S(2)}) async-start(), calls=%async_computation.3 | async-start | bytes 8650752 | tf_op jit(solution)/shard_map/reduce_scatter | solution.py:33
  145.6 317.9 %copy-start.2 = (f32[2,128,512]{2,1,0:T(8,128)S(1)}, f32[2,128,512]{2,1,0:T(8,128)}, u32[]{:S(2)}) copy-start(f32[2,128,512]{2,1,0:T(8,128)} %param.11) | copy-start | bytes 1572868
  145.6 317.9 %copy-start.3 = (f32[2,128,512]{2,1,0:T(8,128)S(1)}, f32[2,128,512]{2,1,0:T(8,128)}, u32[]{:S(2)}) copy-start(f32[2,128,512]{2,1,0:T(8,128)} %param.12) | copy-start | bytes 1572868
  145.6 317.9 %all-reduce.3.cloned.1.call-start = ((), (), s32[]{:S(2)}) async-start(), calls=%async_computation.6 | async-start | bytes 524288 | tf_op jit(solution)/shard_map/psum | solution.py:42
  463.5 1.2 copy-start.5
  464.7 4.2 copy-start.1
  464.7 4.2 copy-start.4
  464.8 4.5 copy-start.6
Sparse Core Ops, SparseCore 0:
  11.8 62.9 all-gather.4
  78.0 58.3 all-gather.2
  140.4 118.9 reduce-scatter.4
  263.3 119.2 reduce-scatter.2
  385.6 77.8 all-reduce.2
where the time goes:
time: 481 us; the launch traced here: 480 us
  waiting for transfers between devices  428 us (89%)
  matrix products  24.5 us (5%)
  between operations  15.3 us (3%)
  other arithmetic  10.6 us (2%)
    reduce_scatter x2, waiting for transfers between devices, on_device(): lax.psum_scatter(lax.dot_general(other_side, coeffs, (((0,), (0,)), ((),...  235 us
    all_gather x2, waiting for transfers between devices, on_device(): shard_piece = lax.all_gather(proj_local, 'fsdp', axis=0, tiled=True)  113 us
    psum x1, waiting for transfers between devices, on_device(): lax.psum(partial_sums.astype(jnp.bfloat16), 'dp').astype(jnp.float32)  79.3 us
    dot_general x2, matrix products, on_device(): lax.dot_general(other_side, coeffs, (((0,), (0,)), ((), ())), preferred_e...  18.9 us
  transfers between devices with their start and end apart: 5, of which 5 were waited for; matrix products, arithmetic and copies ran while one was open for 4% of the time, Pallas kernels for 0%

commit v1 on v0

v1 whole, which is shorter than its diff:
```python
import math

import jax
import jax.numpy as jnp
from jax import lax
from jax.sharding import Mesh, PartitionSpec as P

BETA_ONE = 0.9
BETA_TWO = 0.95
EPSILON = 1e-08
ZH, X, C, Y, ZL = SIZES = (4, 4, 2, 4, 2)
NAMES = ("zh", "x", "core", "y", "zl")
BF16 = jnp.bfloat16
F32 = jnp.float32


def flat_index(zh, x, c, y, zl):
    return (((zh * X + x) * C + c) * Y + y) * ZL + zl


def line_groups(axis_of_core):
    groups = []
    for c in range(C):
        for zh in range(ZH):
            for zl in range(ZL):
                for fixed in range(4):
                    if axis_of_core[c] == "x":
                        groups.append([flat_index(zh, i, c, fixed, zl) for i in range(X)])
                    else:
                        groups.append([flat_index(zh, fixed, c, i, zl) for i in range(Y)])
    return groups


WIDE = line_groups("xy")
NARROW = line_groups("yx")


def swap_lines(v, groups):
    return lax.all_to_all(
        v, NAMES, split_axis=0, concat_axis=0, tiled=True, axis_index_groups=groups
    )


def swap_axes(v, axes):
    return lax.all_to_all(v, axes, split_axis=0, concat_axis=0, tiled=True)


def repeat(v, n):
    return jnp.broadcast_to(v[None], (n,) + v.shape)


def to_partner(v):
    return lax.ppermute(v, "core", [(0, 1), (1, 0)])


def on_device(
    activations, cotangents, weights, projectors, first_moment, second_moment, matrix_settings
):
    mats, rows, rank_max = projectors.shape
    token_total = activations.shape[0] * 256
    grad_scale = 1.0 / math.sqrt(token_total)
    core = lax.axis_index("core")
    y = lax.axis_index("y")
    zl = lax.axis_index("zl")
    live = jnp.arange(rank_max)[None, None, :] < matrix_settings[:, 0][:, None, None]
    half, quarter = rows // ZL, rank_max // Y

    a_far = to_partner(activations)
    c_far = to_partner(lax.dynamic_index_in_dim(cotangents, 1 - core, 0, keepdims=False))
    c_near = lax.dynamic_index_in_dim(cotangents, core, 0, keepdims=False)

    masked = jnp.where(live, projectors, jnp.zeros((), BF16))
    piece = lax.dynamic_slice(masked, (0, zl * half, y * quarter), (mats, half, quarter))
    piece = jnp.broadcast_to(piece[None], (ZH * ZL, mats, half, quarter))
    g = swap_axes(piece.reshape(ZH * ZL * C, half, quarter), ("zh", "zl", "core"))
    g = swap_lines(repeat(g, 4), NARROW)
    g = swap_lines(repeat(g, 4), WIDE)
    g = g.reshape(4, 4, ZH, ZL, C, half, quarter)
    full = jnp.where(
        core == 0, g.transpose(2, 0, 4, 3, 5, 1, 6), g.transpose(2, 1, 4, 3, 5, 0, 6)
    ).reshape(ZH * X * C * rows, rank_max)

    on_inputs = lax.dynamic_index_in_dim(matrix_settings[:, 1], core, 0, keepdims=False) == 0
    partial = 0.0
    for a, b in ((activations, c_near), (a_far, c_far)):
        coeffs = jnp.dot(
            jnp.where(on_inputs, a, b), full, preferred_element_type=F32
        ).astype(BF16)
        partial = partial + lax.dot_general(
            jnp.where(on_inputs, b, a), coeffs, (((0,), (0,)), ((), ())),
            preferred_element_type=F32,
        )
    partial = partial.astype(BF16).reshape(ZH, X, C, ZL, half, Y, quarter)
    full_far = to_partner(full)
    s = jnp.where(
        core == 0,
        partial.transpose(1, 5, 0, 3, 2, 4, 6),
        partial.transpose(5, 1, 0, 3, 2, 4, 6),
    )
    s = swap_lines(s, WIDE)
    s = jnp.sum(s.astype(F32), axis=0).astype(BF16)
    s = swap_lines(s, NARROW)
    s = jnp.sum(s.astype(F32), axis=0).astype(BF16)
    s = swap_axes(s.reshape(ZH * ZL * C, half, quarter), ("zh", "zl", "core"))
    s = jnp.sum(s.astype(F32).reshape(ZH * ZL, mats, half, quarter), axis=0).astype(BF16)
    s = swap_axes(repeat(s, Y * ZL), ("y", "zl"))
    s = s.reshape(Y, ZL, mats, half, quarter).transpose(2, 1, 3, 0, 4)
    projected = s.reshape(mats, rows, rank_max).astype(F32) * grad_scale

    moment_one = jnp.where(live, BETA_ONE * first_moment + (1.0 - BETA_ONE) * projected, 0.0)
    moment_two = jnp.where(
        live, BETA_TWO * second_moment + (1.0 - BETA_TWO) * projected * projected, 0.0
    )
    normalized = jnp.where(
        live, moment_one / (jnp.sqrt(moment_two) + EPSILON), 0.0
    ).astype(BF16)
    updates = []
    for k, proj in ((core, full), (1 - core, full_far)):
        n = lax.dynamic_index_in_dim(normalized, k, 0, keepdims=False)
        updates.append(
            lax.dot_general(n, proj, (((1,), (1,)), ((), ())), preferred_element_type=F32)
        )
    near, far = updates
    update = jnp.where(core == 0, jnp.stack([near, far]), jnp.stack([far, near]))
    return ((weights.astype(F32) - update).astype(BF16), moment_one, moment_two)


def solution(mesh):
    split = Mesh(mesh.devices.reshape(SIZES), NAMES)
    owner = ("zh", "x", "core")
    return jax.shard_map(
        on_device,
        mesh=split,
        in_specs=(
            P(NAMES, None),
            P(None, NAMES, None),
            P(None, owner, None),
            P(None, owner, None),
            P(None, owner, None),
            P(None, owner, None),
            P(),
        ),
        out_specs=(P(None, owner, None), P(None, owner, None), P(None, owner, None)),
        check_vma=False,
    )
```

time: 481 us -> 210 us (0.44)
  waiting for transfers between devices: 428 us -> 43.8 us
  blocking collectives: 0 us -> 73.5 us
  local copies, waits for them, and re-layouts: 1.83 us -> 30.7 us
  between operations: 15.3 us -> 0.8 us
  starting transfers between devices: 0.2 us -> 12.1 us
  other arithmetic: 10.6 us -> 18.3 us
    reduce_scatter x2 -> x0, waiting for transfers between devices: 235 us -> none  [on_device(): lax.psum_scatter(lax.dot_general(other_side, coeffs, (((0,), (0,)), ((),...]
    all_gather x2 -> x0, waiting for transfers between devices: 113 us -> none  [on_device(): shard_piece = lax.all_gather(proj_local, 'fsdp', axis=0, tiled=True)]
    psum x1 -> x0, waiting for transfers between devices: 79.3 us -> none  [on_device(): lax.psum(partial_sums.astype(jnp.bfloat16), 'dp').astype(jnp.float32)]
    all_to_all x0 -> x5, blocking collectives: none -> 73.5 us  [the longest x3 45 us: swap_axes(): return lax.all_to_all(v, axes, split_axis=0, concat_axis=0, tiled=True)]
    all_to_all x0 -> x2, waiting for transfers between devices: none -> 43.8 us  [swap_lines(): lax.all_to_all(v, NAMES, split_axis=0, concat_axis=0, tiled=True, axis_in...]
    all_to_all x0 -> x2, starting transfers between devices: none -> 11.6 us  [swap_lines(): lax.all_to_all(v, NAMES, split_axis=0, concat_axis=0, tiled=True, axis_in...]
    select_n x0 -> x1, local copies, waits for them, and re-layouts: none -> 10.3 us  [on_device(): jnp.where(core == 0, g.transpose(2, 0, 4, 3, 5, 1, 6), g.transpose(2, 1,...]
    select_n x1 -> x3, other arithmetic: 1.69 us -> 10.8 us  [the longest x1 7.39 us: on_device(): jnp.where(core == 0, partial.transpose(1, 5, 0, 3, 2, 4, 6), partial.tran...]
  transfers between devices with their start and end apart: 5 -> 5, of which waited for: 5 -> 2; matrix products, arithmetic and copies ran while one was open for 4% -> 20% of each run, Pallas kernels for 0% -> 0%
where the time goes in v1:
time: 210 us; the launch traced here: 208 us
  blocking collectives  73.5 us (35%)
  waiting for transfers between devices  43.8 us (21%)
  local copies, waits for them, and re-layouts  30.7 us (15%)
  matrix products  28.5 us (14%)
  other arithmetic  18.3 us (9%)
  starting transfers between devices  12.1 us (6%)
    all_to_all x3, blocking collectives, swap_axes(): return lax.all_to_all(v, axes, split_axis=0, concat_axis=0, tiled=True)  45 us
    all_to_all x2, waiting for transfers between devices, swap_lines(): lax.all_to_all(v, NAMES, split_axis=0, concat_axis=0, tiled=True, axis_in...  43.8 us
    all_to_all x2, blocking collectives, swap_lines(): lax.all_to_all(v, NAMES, split_axis=0, concat_axis=0, tiled=True, axis_in...  28.5 us
    dot_general x2, matrix products, on_device(): lax.dot_general(jnp.where(on_inputs, b, a), coeffs, (((0,), (0,)), ((), (...  21 us
    all_to_all x2, starting transfers between devices, swap_lines(): lax.all_to_all(v, NAMES, split_axis=0, concat_axis=0, tiled=True, axis_in...  11.6 us
    select_n x1, local copies, waits for them, and re-layouts, on_device(): jnp.where(core == 0, g.transpose(2, 0, 4, 3, 5, 1, 6), g.transpose(2, 1,...  10.3 us
    dot_general x2, matrix products, on_device(): lax.dot_general(n, proj, (((1,), (1,)), ((), ())), preferred_element_type...  7.49 us
    select_n x1, other arithmetic, on_device(): jnp.where(core == 0, partial.transpose(1, 5, 0, 3, 2, 4, 6), partial.tran...  7.39 us
  transfers between devices with their start and end apart: 5, of which 2 were waited for; matrix products, arithmetic and copies ran while one was open for 20% of the time, Pallas kernels for 0%

profile of v1, /device:TPU:2, one launch (start us, length us, event | category | flops | bytes accessed | tf_op | source)
XLA Modules:
  0.0 207.6 jit_solution(1841047617638060873)
XLA Ops:
  0.6 0.9 fusion.28
  2.5 19.5 %all_to_all.35 = bf16[16,64,128]{2,1,0:T(8,128)(2,1)S(1)} all-to-all(bf16[16,64,128]{2,1,0:T(8,128)(2,1)S(1)} %bitcast.58), channel_id=1, replica_groups=mesh['zh'=4,'x'=4,'core'=2,'y'=4,'zl'=2] {'zh','zl','core'}, dimensions={0} | all-to-all | bytes 524288 | tf_op jit(solution)/shard_map/all_to_all | solution.py:45
  22.2 15.2 %all_to_all.36 = bf16[4,16,64,128]{3,2,1,0:T(8,128)(2,1)S(1)} all-to-all(bf16[4,16,64,128]{3,2,1,0:T(8,128)(2,1)S(1)} %broadcast_in_dim.58), channel_id=1, replica_groups={{0,2,4,6},{16,18,20,22},{32,34,36,38},{48,50,52,54},{1,3,5,7},{17,19,21..., dimensions={0} | all-to-all | bytes 2097152 | tf_op jit(solution)/shard_map/all_to_all | solution.py:39
  37.4 3.0 %broadcast_in_dim.59 = bf16[4,4,16,64,128]{4,3,2,1,0:T(8,128)(2,1)} broadcast(bf16[4,16,64,128]{3,2,1,0:T(8,128)(2,1)S(1)} %all_to_all.36), dimensions={1,2,3,4} | broadcast | bytes 5242880 | tf_op jit(solution)/shard_map/broadcast_in_dim | solution.py:49
  40.4 5.3 %all-to-all-start.2 = ((bf16[4,4,16,64,128]{4,3,2,1,0:T(8,128)(2,1)}), bf16[4,4,16,64,128]{4,3,2,1,0:T(8,128)(2,1)}, u32[]{:S(2)}, u32[]{:S(2)}) async-start(bf16[4,4,16,64,128]{4,3,2,1,0:T(8,128)(2,1)} %broadcast_in_dim.59), calls=%async_computation.2 | async-start | bytes 8388608 | tf_op jit(solution)/shard_map/all_to_all | solution.py:39
  45.8 3.1 %dynamic-slice_bitcast_fusion = bf16[256,4096]{1,0:T(8,128)(2,1)} fusion(bf16[2,256,4096]{2,1,0:T(8,128)(2,1)} %param.8, s32[]{:T(128)S(6)} %select_n.87), kind=kLoop, calls=%fused_computation.16 | loop fusion | bytes 4194308 | tf_op jit(solution)/shard_map/jit(dynamic_index_in_dim)/squeeze | solution.py:69
  49.9 22.2 %all-to-all-done.2 = bf16[4,4,16,64,128]{4,3,2,1,0:T(8,128)(2,1)} async-done(((bf16[4,4,16,64,128]{4,3,2,1,0:T(8,128)(2,1)}), bf16[4,4,16,64,128]{4,3,2,1,0:T(8,128)(2,1)}, u32[]{:S(2)}, u32[]{:S(2)}) %all-to-all-start.2) | async-done | bytes 4194336 | tf_op jit(solution)/shard_map/all_to_all | solution.py:39
  72.2 2.6 %bitcast_select_fusion.1 = bf16[4,4,2,2,64,4,128]{6,4,2,3,0,1,5:T(8,128)(2,1)S(1)} fusion(bf16[4,4,2,2,64,4,128]{6,4,2,3,0,1,5:T(8,128)(2,1)} %bitcast.5, bf16[4,4,4,2,2,64,128]{6,5,4,3,2,1,0:T(8,128)(2,1)} %bitcast.3, pred[]{:T(512)S(6)} %eq.11), kind=kLoop, calls=%fused_computation.8 | loop fusion | flops 2097152 | bytes 12582913 | tf_op jit(solution)/shard_map/jit(_where)/select_n | solution.py:79
  74.8 10.3 %copy.36 = bf16[4,4,2,2,64,4,128]{6,5,4,3,2,1,0:T(4,128)(2,1)} copy(bf16[4,4,2,2,64,4,128]{6,4,2,3,0,1,5:T(8,128)(2,1)S(1)} %bitcast_select_fusion.1) | data formatting | bytes 8388608 | tf_op jit(solution)/shard_map/jit(_where)/select_n | solution.py:79
  85.1 10.4 %fusion.2 = f32[4096,512]{1,0:T(8,128)} fusion(bf16[256,4096]{1,0:T(8,128)(2,1)} %param.7, pred[]{:T(512)} %bitcast, bf16[2,256,4096]{2,1,0:T(8,128)(2,1)} %param.8, s32[]{:T(128)S(6)} %select_n.78, bf16[512,8,4,128]{3,2,1,0:T(4,128)(2,1)} %bitcast.51), kind=kOutput, calls=%fused_computation.11 | convolution fusion | flops 2149711872 | bytes 20973568 | tf_op jit(solution)/shard_map/dot_general | solution.py:89
  95.5 10.6 %add_convert_fusion = bf16[4096,512]{1,0:T(8,128)(2,1)} fusion(f32[4096,512]{1,0:T(8,128)} %fusion.2, bf16[256,4096]{1,0:T(8,128)(2,1)S(1)} %collective-permute-done, bf16[256,4096]{1,0:T(8,128)(2,1)} %collective-permute-done.1, pred[]{:T(512)} %bitcast, bf16[512,8,4,128]{3,2,1,0:T(4,128)(2,1)} %bitcast.52), kind=kOutput, calls=%fused_computation | convolution fusion | flops 2153906176 | bytes 20971520 | tf_op jit(solution)/shard_map/dot_general | solution.py:89
  106.1 6.9 %reshape.80 = bf16[4,4,2,2,64,4,128]{6,5,4,3,2,1,0:T(4,128)(2,1)} reshape(bf16[4096,512]{1,0:T(8,128)(2,1)} %add_convert_fusion) | data formatting | bytes 8388608 | tf_op jit(solution)/shard_map/reshape | solution.py:93
  113.0 7.4 %bitcast_select_fusion = bf16[4,4,4,2,2,64,128]{6,5,3,4,1,2,0:T(8,128)(2,1)} fusion(bf16[4,4,2,2,64,4,128]{6,5,4,3,2,1,0:T(4,128)(2,1)} %reshape.80, pred[]{:T(512)S(6)} %eq.11), kind=kLoop, calls=%fused_computation.7 | loop fusion | flops 2097152 | bytes 8388609 | tf_op jit(solution)/shard_map/jit(_where)/select_n | solution.py:95
  120.4 6.3 %all-to-all-start.3 = ((bf16[4,4,4,2,2,64,128]{6,5,3,4,1,2,0:T(8,128)(2,1)}), bf16[4,4,4,2,2,64,128]{6,5,3,4,1,2,0:T(8,128)(2,1)}, u32[]{:S(2)}, u32[]{:S(2)}) async-start(bf16[4,4,4,2,2,64,128]{6,5,3,4,1,2,0:T(8,128)(2,1)} %bitcast_select_fusion), calls=%async_computation.3 | async-start | bytes 8388608 | tf_op jit(solution)/shard_map/all_to_all | solution.py:39
  126.7 4.8 %copy.57 = bf16[512,8,4,128]{3,1,2,0:T(8,128)(2,1)} copy(bf16[512,8,4,128]{3,2,1,0:T(4,128)(2,1)} %bitcast.53) | data formatting | bytes 8388608
  131.5 21.6 %all-to-all-done.3 = bf16[4,4,4,2,2,64,128]{6,5,3,4,1,2,0:T(8,128)(2,1)} async-done(((bf16[4,4,4,2,2,64,128]{6,5,3,4,1,2,0:T(8,128)(2,1)}), bf16[4,4,4,2,2,64,128]{6,5,3,4,1,2,0:T(8,128)(2,1)}, u32[]{:S(2)}, u32[]{:S(2)}) %all-to-all-start.3) | async-done | bytes 4194336 | tf_op jit(solution)/shard_map/all_to_all | solution.py:39
  153.1 3.3 %reduce_sum.33 = bf16[4,4,2,2,64,128]{5,4,2,3,0,1:T(8,128)(2,1)S(1)} reduce(bf16[4,4,4,2,2,64,128]{6,5,3,4,1,2,0:T(8,128)(2,1)} %all-to-all-done.3, bf16[]{:T(256)} %constant.51.clone.1), dimensions={0}, to_apply=%region_0.1 | reduce | flops 1572864 | bytes 5242882 | tf_op jit(solution)/shard_map/reduce_sum | solution.py:101
  156.5 13.3 %all_to_all.37 = bf16[4,4,2,2,64,128]{5,4,2,3,1,0:T(8,128)(2,1)S(1)} all-to-all(bf16[4,4,2,2,64,128]{5,4,2,3,1,0:T(8,128)(2,1)S(1)} %copy.40), channel_id=1, replica_groups={{0,2,4,6},{16,18,20,22},{32,34,36,38},{48,50,52,54},{1,3,5,7},{17,19,21..., dimensions={0} | all-to-all | bytes 2097152 | tf_op jit(solution)/shard_map/all_to_all | solution.py:39
  170.1 14.5 %all_to_all.38 = bf16[16,64,128]{2,1,0:T(8,128)(2,1)S(1)} all-to-all(bf16[16,64,128]{2,1,0:T(8,128)(2,1)S(1)} %bitcast.59), channel_id=1, replica_groups=mesh['zh'=4,'x'=4,'core'=2,'y'=4,'zl'=2] {'zh','zl','core'}, dimensions={0} | all-to-all | bytes 524288 | tf_op jit(solution)/shard_map/all_to_all | solution.py:45
  184.7 11.0 %all_to_all.39 = bf16[8,2,64,128]{3,2,1,0:T(8,128)(2,1)S(1)} all-to-all(bf16[8,2,64,128]{3,2,1,0:T(8,128)(2,1)S(1)} %broadcast_in_dim.60), channel_id=1, replica_groups=mesh['zh'=4,'x'=4,'core'=2,'y'=4,'zl'=2] {'y','zl'}, dimensions={0} | all-to-all | bytes 524288 | tf_op jit(solution)/shard_map/all_to_all | solution.py:45
  196.9 1.3 select_convert_fusion
  198.2 3.7 %convolution_bitcast_fusion.1 = f32[1,128,4096]{2,1,0:T(8,128)S(1)} fusion(bf16[2,128,512]{2,1,0:T(8,128)(2,1)S(1)} %get-tuple-element.3, s32[]{:T(128)S(6)} %select_n.78, bf16[512,8,4,128]{3,2,1,0:T(4,128)(2,1)} %bitcast.54), kind=kOutput, calls=%fused_computation.2 | convolution fusion | flops 536870912 | bytes 6422532 | tf_op jit(solution)/shard_map/dot_general | solution.py:121
  201.9 3.8 %convolution_bitcast_fusion = f32[1,128,4096]{2,1,0:T(8,128)S(1)} fusion(bf16[4096,512]{1,0:T(8,128)(2,1)} %collective-permute-done.2, bf16[2,128,512]{2,1,0:T(8,128)(2,1)S(1)} %get-tuple-element.3, s32[]{:T(128)S(6)} %select_n.87), kind=kOutput, calls=%fused_computation.1 | convolution fusion | flops 536870912 | bytes 6422532 | tf_op jit(solution)/shard_map/dot_general | solution.py:121
  205.7 1.9 fusion.1
  (28 shorter events, 3.8 us)
Async XLA Ops:
  40.4 31.7 %all-to-all-start.2 = ((bf16[4,4,16,64,128]{4,3,2,1,0:T(8,128)(2,1)}), bf16[4,4,16,64,128]{4,3,2,1,0:T(8,128)(2,1)}, u32[]{:S(2)}, u32[]{:S(2)}) async-start(bf16[4,4,16,64,128]{4,3,2,1,0:T(8,128)(2,1)} %broadcast_in_dim.59), calls=%async_computation.2 | async-start | bytes 8388608 | tf_op jit(solution)/shard_map/all_to_all | solution.py:39
  48.9 46.6 %collective-permute-start = (bf16[256,4096]{1,0:T(8,128)(2,1)}, bf16[256,4096]{1,0:T(8,128)(2,1)S(1)}, u32[]{:S(2)}, u32[]{:S(2)}) collective-permute-start(bf16[256,4096]{1,0:T(8,128)(2,1)} %dynamic-slice_bitcast_fusion), channel_id=1, source_target_pairs={{0,8},{8,0},{1,9},{9,1},{2,10},{10,2},{3,11},{11,3},{4,12},{12,4},... | collective-permute-start | bytes 6291464 | tf_op jit(solution)/shard_map/ppermute | solution.py:53
  48.9 46.6 %collective-permute-start.1 = (bf16[256,4096]{1,0:T(8,128)(2,1)}, bf16[256,4096]{1,0:T(8,128)(2,1)}, u32[]{:S(2)}, u32[]{:S(2)}) collective-permute-start(bf16[256,4096]{1,0:T(8,128)(2,1)} %param.7), channel_id=1, source_target_pairs={{0,8},{8,0},{1,9},{9,1},{2,10},{10,2},{3,11},{11,3},{4,12},{12,4},... | collective-permute-start | bytes 6291464 | tf_op jit(solution)/shard_map/ppermute | solution.py:53
  120.4 32.7 %all-to-all-start.3 = ((bf16[4,4,4,2,2,64,128]{6,5,3,4,1,2,0:T(8,128)(2,1)}), bf16[4,4,4,2,2,64,128]{6,5,3,4,1,2,0:T(8,128)(2,1)}, u32[]{:S(2)}, u32[]{:S(2)}) async-start(bf16[4,4,4,2,2,64,128]{6,5,3,4,1,2,0:T(8,128)(2,1)} %bitcast_select_fusion), calls=%async_computation.3 | async-start | bytes 8388608 | tf_op jit(solution)/shard_map/all_to_all | solution.py:39
  131.5 70.4 %collective-permute-start.2 = (bf16[4096,512]{1,0:T(8,128)(2,1)}, bf16[4096,512]{1,0:T(8,128)(2,1)}, u32[]{:S(2)}, u32[]{:S(2)}) collective-permute-start(bf16[4096,512]{1,0:T(8,128)(2,1)} %bitcast.50), channel_id=1, source_target_pairs={{0,8},{8,0},{1,9},{9,1},{2,10},{10,2},{3,11},{11,3},{4,12},{12,4},... | collective-permute-start | bytes 12582920 | tf_op jit(solution)/shard_map/ppermute | solution.py:53
  169.8 27.0 %copy-start.1 = (f32[2,128,512]{2,1,0:T(8,128)S(1)}, f32[2,128,512]{2,1,0:T(8,128)}, u32[]{:S(2)}) copy-start(f32[2,128,512]{2,1,0:T(8,128)} %param.12) | copy-start | bytes 1572868
  169.8 27.1 %copy-start.2 = (f32[2,128,512]{2,1,0:T(8,128)S(1)}, f32[2,128,512]{2,1,0:T(8,128)}, u32[]{:S(2)}) copy-start(f32[2,128,512]{2,1,0:T(8,128)} %param.11) | copy-start | bytes 1572868
  201.9 3.8 %copy-start = (bf16[2,128,4096]{2,1,0:T(8,128)(2,1)S(1)}, bf16[2,128,4096]{2,1,0:T(8,128)(2,1)}, u32[]{:S(2)}) copy-start(bf16[2,128,4096]{2,1,0:T(8,128)(2,1)} %param.9) | copy-start | bytes 6291460

commit v2 on v1

v2 whole, which is shorter than its diff:
```python
import functools
import math

import jax
import jax.numpy as jnp
from jax import lax
from jax.experimental import pallas as pl
from jax.experimental.pallas import tpu as pltpu
from jax.sharding import Mesh, PartitionSpec as P


BETA_ONE = 0.9
BETA_TWO = 0.95
EPSILON = 1e-08
ZH, X, C, Y, ZL = SIZES = (4, 4, 2, 4, 2)
NAMES = ("zh", "x", "core", "y", "zl")
BF16 = jnp.bfloat16
F32 = jnp.float32
VMEM = pltpu.MemorySpace.VMEM
SMEM = pltpu.MemorySpace.SMEM
PARAMS = pltpu.CompilerParams(vmem_limit_bytes=28 << 20)


def flat_index(zh, x, c, y, zl):
    return (((zh * X + x) * C + c) * Y + y) * ZL + zl


def line_groups(axis_of_core):
    groups = []
    for c in range(C):
        for zh in range(ZH):
            for zl in range(ZL):
                for fixed in range(4):
                    if axis_of_core[c] == "x":
                        groups.append([flat_index(zh, i, c, fixed, zl) for i in range(X)])
                    else:
                        groups.append([flat_index(zh, fixed, c, i, zl) for i in range(Y)])
    return groups


WIDE = line_groups("xy")
NARROW = line_groups("yx")


def shift(v, groups, offset):
    pairs = [(g[i], g[(i + offset) % 4]) for g in groups for i in range(4)]
    return lax.ppermute(v, NAMES, pairs)


def swap_lines(v, groups):
    return lax.all_to_all(
        v, NAMES, split_axis=0, concat_axis=0, tiled=True, axis_index_groups=groups
    )


def swap_axes(v, axes):
    return lax.all_to_all(v, axes, split_axis=0, concat_axis=0, tiled=True)


def repeat(v, n):
    return jnp.broadcast_to(v[None], (n,) + v.shape)


def to_partner(v):
    return lax.ppermute(v, "core", [(0, 1), (1, 0)])


def place(core, a, b):
    first = core == 0
    return jnp.where(first, a, b), jnp.where(first, b, a)


def coeffs_kernel(count, first, last, pos, x_ref, *refs):
    blocks, refs = refs[:count], refs[count:]
    acc = refs[-1]
    if first:
        acc[...] = jnp.zeros_like(acc)
    else:
        acc[...] = refs[0][...]
    for i in range(count):
        for b in range(4):
            x, y = place(pos[0], pos[1 + i], b)
            lhs = jnp.concatenate(
                [
                    x_ref[:, pl.ds(pl.multiple_of((zh * X + x) * 256, 256), 256)]
                    for zh in range(ZH)
                ],
                axis=1,
            )
            rhs = blocks[i][b].reshape(ZH * 256, 128)
            acc[y] += jnp.dot(lhs, rhs, preferred_element_type=F32)
    if last:
        refs[-2][...] = acc[...].astype(BF16)


def coeffs_step(pos, x, blocks, acc=None, last=False):
    tokens = x.shape[0]
    shape = (4, tokens, 128)
    ins = [pos, x, *blocks] + ([] if acc is None else [acc])
    return pl.pallas_call(
        functools.partial(coeffs_kernel, len(blocks), acc is None, last),
        out_shape=jax.ShapeDtypeStruct(shape, BF16 if last else F32),
        in_specs=[pl.BlockSpec(memory_space=SMEM)]
        + [pl.BlockSpec(memory_space=VMEM)] * (len(ins) - 1),
        out_specs=pl.BlockSpec(memory_space=VMEM),
        scratch_shapes=[pltpu.VMEM(shape, F32)] if last else [],
        compiler_params=PARAMS,
        name="coeffs",
    )(*ins)


def grad_kernel(pos, xt_ref, coeffs_ref, out_ref):
    for b in range(4):
        x, y = place(pos[0], pos[1], b)
        lhs = jnp.concatenate([xt_ref[zh, x] for zh in range(ZH)], axis=0)
        part = jnp.dot(lhs, coeffs_ref[y], preferred_element_type=F32)
        out_ref[b] = part.astype(BF16).reshape(ZH, 256, 128)


def grad_block(pos, xt, coeffs):
    return pl.pallas_call(
        grad_kernel,
        out_shape=jax.ShapeDtypeStruct((4, ZH, 256, 128), BF16),
        in_specs=[pl.BlockSpec(memory_space=SMEM)] + [pl.BlockSpec(memory_space=VMEM)] * 2,
        out_specs=pl.BlockSpec(memory_space=VMEM),
        compiler_params=PARAMS,
        name="grads",
    )(pos, xt, coeffs)


def order_kernel(pos, *refs):
    out_ref = refs[4]
    for i in range(4):
        for b in range(4):
            x, y = place(pos[0], pos[1 + i], b)
            for zh in range(ZH):
                lanes = pl.ds(pl.multiple_of((zh * X + x) * 256, 256), 256)
                out_ref[y, :, lanes] = refs[i][b, zh].T


def in_order(pos, blocks):
    return pl.pallas_call(
        order_kernel,
        out_shape=jax.ShapeDtypeStruct((Y, 128, ZH * X * 256), BF16),
        in_specs=[pl.BlockSpec(memory_space=SMEM)] + [pl.BlockSpec(memory_space=VMEM)] * 4,
        out_specs=pl.BlockSpec(memory_space=VMEM),
        compiler_params=PARAMS,
        name="order",
    )(pos, *blocks)


def sides_kernel(pos, a_near, a_far, c_near, c_far, x_ref, xt_ref):
    tokens = a_near.shape[0]

    def write(projected, other):
        x_ref[:tokens, :] = projected[0]
        x_ref[tokens:, :] = projected[1]
        xt_ref[:, :tokens] = other[0].T
        xt_ref[:, tokens:] = other[1].T

    a = lambda: (a_near[...], a_far[...])
    c = lambda: (c_near[0], c_far[...])

    @pl.when(pos[1] == 0)
    def _():
        write(a(), c())

    @pl.when(pos[1] != 0)
    def _():
        write(c(), a())


def make_sides(pos, a_near, a_far, cotangents, c_far):
    tokens, features = a_near.shape
    chunk = 512
    block = pl.BlockSpec((tokens, chunk), lambda j, pos: (0, j))
    return pl.pallas_call(
        sides_kernel,
        out_shape=(
            jax.ShapeDtypeStruct((2 * tokens, features), BF16),
            jax.ShapeDtypeStruct((features, 2 * tokens), BF16),
        ),
        grid_spec=pltpu.PrefetchScalarGridSpec(
            num_scalar_prefetch=1,
            grid=(features // chunk,),
            in_specs=[
                block,
                block,
                pl.BlockSpec((1, tokens, chunk), lambda j, pos: (pos[0], 0, j)),
                block,
            ],
            out_specs=(
                pl.BlockSpec((2 * tokens, chunk), lambda j, pos: (0, j)),
                pl.BlockSpec((chunk, 2 * tokens), lambda j, pos: (j, 0)),
            ),
        ),
        compiler_params=PARAMS,
        name="sides",
    )(pos, a_near, a_far, cotangents, c_far)


def update_kernel(
    scale, pos, settings, s_ref, m1_ref, m2_ref, near_ref, far_ref, w_ref,
    w_out, m1_out, m2_out, n_ref,
):
    mats = m1_ref.shape[0]
    half, quarter = s_ref.shape[3:]
    for k in range(mats):
        for y in range(Y):
            columns = slice(y * quarter, (y + 1) * quarter)
            column = lax.broadcasted_iota(jnp.int32, (half, quarter), 1) + y * quarter
            live = column < settings[k, 0]
            for z in range(ZL):
                rows = slice(z * half, (z + 1) * half)
                grad = s_ref[y, z, k].astype(F32) * scale
                m1 = BETA_ONE * m1_ref[k, rows, columns] + (1.0 - BETA_ONE) * grad
                m2 = BETA_TWO * m2_ref[k, rows, columns] + (1.0 - BETA_TWO) * grad * grad
                m1 = jnp.where(live, m1, 0.0)
                m2 = jnp.where(live, m2, 0.0)
                m1_out[k, rows, columns] = m1
                m2_out[k, rows, columns] = m2
                normalized = jnp.where(live, m1 / (jnp.sqrt(m2) + EPSILON), 0.0)
                n_ref[k, rows, columns] = normalized.astype(BF16)
    for k, p_ref in ((pos[0], near_ref), (1 - pos[0], far_ref)):
        n = n_ref[k]
        for j in range(0, w_ref.shape[2], 512):
            lanes = slice(j, j + 512)
            rhs = p_ref[:, :, lanes].reshape(Y * quarter, 512)
            update = jnp.dot(n, rhs, preferred_element_type=F32)
            w_out[k, :, lanes] = (w_ref[k, :, lanes].astype(F32) - update).astype(BF16)


def apply_update(scale, pos, settings, s, m1, m2, near, far, weights):
    return pl.pallas_call(
        functools.partial(update_kernel, scale),
        out_shape=(
            jax.ShapeDtypeStruct(weights.shape, BF16),
            jax.ShapeDtypeStruct(m1.shape, F32),
            jax.ShapeDtypeStruct(m2.shape, F32),
        ),
        in_specs=[pl.BlockSpec(memory_space=SMEM)] * 2
        + [pl.BlockSpec(memory_space=VMEM)] * 6,
        out_specs=(pl.BlockSpec(memory_space=VMEM),) * 3,
        scratch_shapes=[pltpu.VMEM(m1.shape, BF16)],
        compiler_params=PARAMS,
        name="update",
    )(pos, settings, s, m1, m2, near, far, weights)


def on_device(
    activations, cotangents, weights, projectors, first_moment, second_moment, matrix_settings
):
    mats, rows, rank_max = projectors.shape
    token_total = activations.shape[0] * 256
    grad_scale = 1.0 / math.sqrt(token_total)
    core = lax.axis_index("core")
    y = lax.axis_index("y")
    zl = lax.axis_index("zl")
    mine = jnp.where(core == 0, lax.axis_index("x"), y)
    live = jnp.arange(rank_max)[None, None, :] < matrix_settings[:, 0][:, None, None]
    half, quarter = rows // ZL, rank_max // Y

    def positions(*offsets):
        return jnp.stack([core] + [(mine + o) % 4 for o in offsets]).astype(jnp.int32)

    far_index = 1 - core
    a_far = to_partner(activations)
    c_far = to_partner(lax.dynamic_index_in_dim(cotangents, far_index, 0, keepdims=False))

    masked = jnp.where(live, projectors, jnp.zeros((), BF16))
    piece = lax.dynamic_slice(masked, (0, zl * half, y * quarter), (mats, half, quarter))
    piece = jnp.broadcast_to(piece[None, :, None], (ZH, mats, ZL, half, quarter))
    g = swap_axes(piece.reshape(ZH * C * ZL, half, quarter), ("zh", "core", "zl"))
    g = swap_lines(repeat(g.reshape(ZH, 256, quarter), 4), NARROW)
    g = g.reshape(4, ZH, 256, quarter)
    by_offset = {0: g}
    for o in (1, 3, 2):
        by_offset[o] = shift(g, WIDE, o)

    side = lax.dynamic_index_in_dim(matrix_settings[:, 1], core, 0, keepdims=False)
    projected_side, other_side = make_sides(
        jnp.stack([core, side]).astype(jnp.int32), activations, a_far, cotangents, c_far
    )
    other_side = other_side.reshape(ZH, X, 256, 512)

    acc = coeffs_step(positions(0), projected_side, [g])
    acc = coeffs_step(positions(-1, -3), projected_side, [by_offset[1], by_offset[3]], acc)
    coeffs = coeffs_step(positions(-2), projected_side, [by_offset[2]], acc, last=True)

    parts = []
    for o in (2, 1, 3):
        block = grad_block(positions(o), other_side, coeffs)
        parts.append(shift(block, WIDE, o))
    s = grad_block(positions(0), other_side, coeffs)
    full = in_order(positions(0, -1, -2, -3), [by_offset[o] for o in range(4)])
    full_far = to_partner(full)
    s = s.astype(F32)
    for part in parts:
        s = s + part.astype(F32)

    s = swap_lines(s.astype(BF16), NARROW).reshape(4, ZH, 256, quarter)
    s = jnp.sum(s.astype(F32), axis=0).astype(BF16)
    s = swap_axes(s.reshape(ZH * C * ZL, half, quarter), ("zh", "core", "zl"))
    s = s.astype(F32).reshape(ZH, mats, ZL, half, quarter)
    s = jnp.sum(s, axis=(0, 2)).astype(BF16)
    s = swap_axes(repeat(s, Y * ZL), ("y", "zl"))
    return apply_update(
        grad_scale,
        positions(),
        matrix_settings,
        s.reshape(Y, ZL, mats, half, quarter),
        first_moment,
        second_moment,
        full,
        full_far,
        weights,
    )


def solution(mesh):
    split = Mesh(mesh.devices.reshape(SIZES), NAMES)
    owner = ("zh", "x", "core")
    return jax.shard_map(
        on_device,
        mesh=split,
        in_specs=(
            P(NAMES, None),
            P(None, NAMES, None),
            P(None, owner, None),
            P(None, owner, None),
            P(None, owner, None),
            P(None, owner, None),
            P(),
        ),
        out_specs=(P(None, owner, None), P(None, owner, None), P(None, owner, None)),
        check_vma=False,
    )
```

time: 210 us -> 168 us (0.80)
  Pallas kernels: 0 us -> 31.9 us
  matrix products: 28.5 us -> 0 us
  local copies, waits for them, and re-layouts: 30.7 us -> 8.14 us
  blocking collectives: 73.5 us -> 58.6 us
  other arithmetic: 18.3 us -> 5.01 us
  waiting for transfers between devices: 43.8 us -> 49.6 us
    ppermute x0 -> x6, waiting for transfers between devices: none -> 38.7 us  [shift(): return lax.ppermute(v, NAMES, pairs)]
    all_to_all x2 -> x1, waiting for transfers between devices: 43.8 us -> 10.9 us  [swap_lines(): lax.all_to_all(v, NAMES, split_axis=0, concat_axis=0, tiled=True, axis_in...]
    pallas_call x0 -> x10, Pallas kernels: none -> 31.9 us  [the longest x3 7.44 us: coeffs_step(): pl.pallas_call(functools.partial(coeffs_kernel, len(blocks), acc is None,...]
    dot_general x4 -> x0, matrix products: 28.5 us -> none  [the longest x2 21 us: on_device(): lax.dot_general(jnp.where(on_inputs, b, a), coeffs, (((0,), (0,)), ((), (...]
    all_to_all x2 -> x1, blocking collectives: 28.5 us -> 14.3 us  [swap_lines(): lax.all_to_all(v, NAMES, split_axis=0, concat_axis=0, tiled=True, axis_in...]
    select_n x1 -> x0, local copies, waits for them, and re-layouts: 10.3 us -> none  [on_device(): jnp.where(core == 0, g.transpose(2, 0, 4, 3, 5, 1, 6), g.transpose(2, 1,...]
    select_n x2 -> x0, other arithmetic: 10 us -> none  [the longest x1 7.39 us: on_device(): jnp.where(core == 0, partial.transpose(1, 5, 0, 3, 2, 4, 6), partial.tran...]
    ppermute x0 -> x6, starting transfers between devices: none -> 7.99 us  [shift(): return lax.ppermute(v, NAMES, pairs)]
  transfers between devices with their start and end apart: 5 -> 10, of which waited for: 2 -> 7; matrix products, arithmetic and copies ran while one was open for 20% -> 5% of each run, Pallas kernels for 0% -> 15%
where the time goes in v2:
time: 168 us; the launch traced here: 167 us
  blocking collectives  58.6 us (35%)
  waiting for transfers between devices  49.6 us (30%)
  Pallas kernels  31.9 us (19%)
  starting transfers between devices  13 us (8%)
  local copies, waits for them, and re-layouts  8.14 us (5%)
  other arithmetic  5.01 us (3%)
    all_to_all x3, blocking collectives, swap_axes(): return lax.all_to_all(v, axes, split_axis=0, concat_axis=0, tiled=True)  44.3 us
    ppermute x6, waiting for transfers between devices, shift(): return lax.ppermute(v, NAMES, pairs)  38.7 us
    all_to_all x1, blocking collectives, swap_lines(): lax.all_to_all(v, NAMES, split_axis=0, concat_axis=0, tiled=True, axis_in...  14.3 us
    all_to_all x1, waiting for transfers between devices, swap_lines(): lax.all_to_all(v, NAMES, split_axis=0, concat_axis=0, tiled=True, axis_in...  10.9 us
    ppermute x6, starting transfers between devices, shift(): return lax.ppermute(v, NAMES, pairs)  7.99 us
    pallas_call x3, Pallas kernels, coeffs_step(): pl.pallas_call(functools.partial(coeffs_kernel, len(blocks), acc is None,...  7.44 us
    pallas_call x4, Pallas kernels, grad_block(): pl.pallas_call(grad_kernel, out_shape=jax.ShapeDtypeStruct((4, ZH, 256, 1...  7.21 us
    pallas_call x1, Pallas kernels, apply_update(): pl.pallas_call(functools.partial(update_kernel, scale), out_shape=(jax.Sh...  6.51 us
  transfers between devices with their start and end apart: 10, of which 7 were waited for; matrix products, arithmetic and copies ran while one was open for 5% of the time, Pallas kernels for 15%

profile of v2, /device:TPU:2, one launch (start us, length us, event | category | flops | bytes accessed | tf_op | source)
XLA Modules:
  0.0 167.1 jit_solution(12317797638990489762)
XLA Ops:
  2.5 18.8 %all_to_all.25 = bf16[16,64,128]{2,1,0:T(8,128)(2,1)S(1)} all-to-all(bf16[16,64,128]{2,1,0:T(8,128)(2,1)S(1)} %bitcast.25), channel_id=1, replica_groups=mesh['zh'=4,'x'=4,'core'=2,'y'=4,'zl'=2] {'zh','core','zl'}, dimensions={0} | all-to-all | bytes 524288 | tf_op jit(solution)/shard_map/all_to_all | solution.py:57
  22.4 4.5 %all-to-all-start.1 = ((bf16[4,4,256,128]{3,2,1,0:T(8,128)(2,1)}), bf16[4,4,256,128]{3,2,1,0:T(8,128)(2,1)S(1)}, u32[]{:S(2)}, u32[]{:S(2)}) async-start(bf16[4,4,256,128]{3,2,1,0:T(8,128)(2,1)} %broadcast_in_dim.36), calls=%async_computation.1 | async-start | bytes 2097152 | tf_op jit(solution)/shard_map/all_to_all | solution.py:51
  26.9 10.9 %all-to-all-done.1.refs_0_ = bf16[4,4,256,128]{3,2,1,0:T(8,128)(2,1)S(1)} async-done(((bf16[4,4,256,128]{3,2,1,0:T(8,128)(2,1)}), bf16[4,4,256,128]{3,2,1,0:T(8,128)(2,1)S(1)}, u32[]{:S(2)}, u32[]{:S(2)}) %all-to-all-start.1) | async-done | bytes 1048608 | tf_op jit(solution)/shard_map/all_to_all | solution.py:51
  39.8 2.1 %collective-permute-start.2 = (bf16[4,4,256,128]{3,2,1,0:T(8,128)(2,1)S(1)}, bf16[4,4,256,128]{3,2,1,0:T(8,128)(2,1)}, u32[]{:S(2)}, u32[]{:S(2)}) collective-permute-start(bf16[4,4,256,128]{3,2,1,0:T(8,128)(2,1)S(1)} %all-to-all-done.1.refs_0_), channel_id=1, source_target_pairs={{0,32},{16,48},{32,0},{48,16},{2,34},{18,50},{34,2},{50,18},{4,36}... | collective-permute-start | bytes 3145736 | tf_op jit(solution)/shard_map/ppermute | solution.py:47
  41.9 3.1 %dynamic-slice_bitcast_fusion = bf16[256,4096]{1,0:T(8,128)(2,1)} fusion(bf16[2,256,4096]{2,1,0:T(8,128)(2,1)} %c_near.1, s32[]{:T(128)S(6)} %select_n.65), kind=kLoop, calls=%fused_computation.1 | loop fusion | bytes 4194308 | tf_op jit(solution)/shard_map/jit(dynamic_index_in_dim)/squeeze | solution.py:268
  45.7 6.9 %collective-permute-done.3.refs_0_.refs_1_ = bf16[4,4,256,128]{3,2,1,0:T(8,128)(2,1)S(1)} collective-permute-done((bf16[4,4,256,128]{3,2,1,0:T(8,128)(2,1)S(1)}, bf16[4,4,256,128]{3,2,1,0:T(8,128)(2,1)S(1)}, u32[]{:S(2)}, u32[]{:S(2)}) %collective-permute-start.3) | collective-permute-done | bytes 1048608 | tf_op jit(solution)/shard_map/ppermute | solution.py:47
  54.1 12.0 %collective-permute-done.2.refs_0_.refs_2_ = bf16[4,4,256,128]{3,2,1,0:T(8,128)(2,1)} collective-permute-done((bf16[4,4,256,128]{3,2,1,0:T(8,128)(2,1)S(1)}, bf16[4,4,256,128]{3,2,1,0:T(8,128)(2,1)}, u32[]{:S(2)}, u32[]{:S(2)}) %collective-permute-start.2) | collective-permute-done | bytes 1048608 | tf_op jit(solution)/shard_map/ppermute | solution.py:47
  66.0 4.3 %order.1.near_ref = bf16[4,128,4096]{2,1,0:T(8,128)(2,1)} custom-call(s32[5]{0:T(128)S(1)} %stack.79.pos, bf16[4,4,256,128]{3,2,1,0:T(8,128)(2,1)S(1)} %all-to-all-done.1.refs_0_, bf16[4,4,256,128]{3,2,1,0:T(8,128)(2,1)S(1)} %collective-permute-done.3.refs_0_.refs_1_, bf16[4,4,256,128]{3,2,1,0:T(8,128)(2,1)} %collective-permute-done.2.refs_0_.refs_2_, ...), custom_call_target="tpu_custom_call" | custom-call | tf_op jit(solution)/shard_map/order/pallas_call | solution.py:142
  72.0 2.2 %copy-done = bf16[2,256,4096]{2,1,0:T(8,128)(2,1)S(1)} copy-done((bf16[2,256,4096]{2,1,0:T(8,128)(2,1)S(1)}, bf16[2,256,4096]{2,1,0:T(8,128)(2,1)}, u32[]{:S(2)}) %copy-start) | copy-done | bytes 4194328
  74.2 6.4 %sides.1 = (bf16[512,4096]{1,0:T(8,128)(2,1)S(1)}, bf16[4096,512]{1,0:T(8,128)(2,1)S(1)}) custom-call(s32[2]{0:T(128)S(1)} %pad_add_fusion.1.pos, bf16[256,4096]{1,0:T(8,128)(2,1)} %a_near.1, bf16[256,4096]{1,0:T(8,128)(2,1)} %collective-permute-done.a_far, bf16[2,256,4096]{2,1,0:T(8,128)(2,1)S(1)} %copy-done, bf16[256,4096]{1,0:T(8,128)(2,1)} %collective-permute-done.1.c_far), custom_call_target="tpu_custom_call" | custom-call | tf_op jit(solution)/shard_map/sides/pallas_call | solution.py:177
  80.6 1.9 %coeffs.3.refs_2_ = f32[4,512,128]{2,1,0:T(8,128)S(1)} custom-call(s32[2]{0:T(128)S(1)} %get-tuple-element.9.pos, bf16[512,4096]{1,0:T(8,128)(2,1)S(1)} %get-tuple-element.6.x_ref, bf16[4,4,256,128]{3,2,1,0:T(8,128)(2,1)S(1)} %all-to-all-done.1.refs_0_), custom_call_target="tpu_custom_call" | custom-call | tf_op jit(solution)/shard_map/coeffs/pallas_call | solution.py:100
  82.5 3.0 %coeffs.4.refs_1_ = f32[4,512,128]{2,1,0:T(8,128)S(1)} custom-call(s32[3]{0:T(128)S(1)} %pad_add_fusion.3.pos, bf16[512,4096]{1,0:T(8,128)(2,1)S(1)} %get-tuple-element.6.x_ref, bf16[4,4,256,128]{3,2,1,0:T(8,128)(2,1)S(1)} %collective-permute-done.3.refs_0_.refs_1_, bf16[4,4,256,128]{3,2,1,0:T(8,128)(2,1)S(1)} %collective-permute-done.4.refs_1_.refs_3_, ...), custom_call_target="tpu_custom_call" | custom-call | tf_op jit(solution)/shard_map/coeffs/pallas_call | solution.py:100
  85.5 2.6 %coeffs.5.coeffs_ref = bf16[4,512,128]{2,1,0:T(8,128)(2,1)S(1)} custom-call(s32[2]{0:T(128)S(1)} %get-tuple-element.10.pos, bf16[512,4096]{1,0:T(8,128)(2,1)S(1)} %get-tuple-element.6.x_ref, bf16[4,4,256,128]{3,2,1,0:T(8,128)(2,1)} %collective-permute-done.2.refs_0_.refs_2_, f32[4,512,128]{2,1,0:T(8,128)S(1)} %coeffs.4.refs_1_), custom_call_target="tpu_custom_call" | custom-call | tf_op jit(solution)/shard_map/coeffs/pallas_call | solution.py:100
  88.1 1.8 %grads.5 = bf16[4,4,256,128]{3,2,1,0:T(8,128)(2,1)S(1)} custom-call(s32[2]{0:T(128)S(1)} %pad_add_fusion.4.pos, bf16[4,4,256,512]{3,2,1,0:T(8,128)(2,1)S(1)} %bitcast.17, bf16[4,512,128]{2,1,0:T(8,128)(2,1)S(1)} %coeffs.5.coeffs_ref), custom_call_target="tpu_custom_call" | custom-call | tf_op jit(solution)/shard_map/grads/pallas_call | solution.py:121
  91.6 1.8 %grads.6 = bf16[4,4,256,128]{3,2,1,0:T(8,128)(2,1)S(1)} custom-call(s32[2]{0:T(128)S(1)} %pad_add_fusion.5.pos, bf16[4,4,256,512]{3,2,1,0:T(8,128)(2,1)S(1)} %bitcast.18, bf16[4,512,128]{2,1,0:T(8,128)(2,1)S(1)} %coeffs.5.coeffs_ref), custom_call_target="tpu_custom_call" | custom-call | tf_op jit(solution)/shard_map/grads/pallas_call | solution.py:121
  93.9 1.8 %grads.7 = bf16[4,4,256,128]{3,2,1,0:T(8,128)(2,1)S(1)} custom-call(s32[2]{0:T(128)S(1)} %pad_add_fusion.6.pos, bf16[4,4,256,512]{3,2,1,0:T(8,128)(2,1)S(1)} %bitcast.19, bf16[4,512,128]{2,1,0:T(8,128)(2,1)S(1)} %coeffs.5.coeffs_ref), custom_call_target="tpu_custom_call" | custom-call | tf_op jit(solution)/shard_map/grads/pallas_call | solution.py:121
  97.4 1.8 %grads.4 = bf16[4,4,256,128]{3,2,1,0:T(8,128)(2,1)S(1)} custom-call(s32[2]{0:T(128)S(1)} %get-tuple-element.9.pos, bf16[4,4,256,512]{3,2,1,0:T(8,128)(2,1)S(1)} %bitcast.20, bf16[4,512,128]{2,1,0:T(8,128)(2,1)S(1)} %coeffs.5.coeffs_ref), custom_call_target="tpu_custom_call" | custom-call | tf_op jit(solution)/shard_map/grads/pallas_call | solution.py:121
  99.2 7.2 %collective-permute-done.5 = bf16[4,4,256,128]{3,2,1,0:T(8,128)(2,1)S(1)} collective-permute-done((bf16[4,4,256,128]{3,2,1,0:T(8,128)(2,1)S(1)}, bf16[4,4,256,128]{3,2,1,0:T(8,128)(2,1)S(1)}, u32[]{:S(2)}, u32[]{:S(2)}) %collective-permute-start.5) | collective-permute-done | bytes 1048608 | tf_op jit(solution)/shard_map/ppermute | solution.py:47
  106.4 9.1 %collective-permute-done.6 = bf16[4,4,256,128]{3,2,1,0:T(8,128)(2,1)S(1)} collective-permute-done((bf16[4,4,256,128]{3,2,1,0:T(8,128)(2,1)S(1)}, bf16[4,4,256,128]{3,2,1,0:T(8,128)(2,1)S(1)}, u32[]{:S(2)}, u32[]{:S(2)}) %collective-permute-start.6) | collective-permute-done | bytes 1048608 | tf_op jit(solution)/shard_map/ppermute | solution.py:47
  115.5 2.1 %collective-permute-done.7 = bf16[4,4,256,128]{3,2,1,0:T(8,128)(2,1)S(1)} collective-permute-done((bf16[4,4,256,128]{3,2,1,0:T(8,128)(2,1)S(1)}, bf16[4,4,256,128]{3,2,1,0:T(8,128)(2,1)S(1)}, u32[]{:S(2)}, u32[]{:S(2)}) %collective-permute-start.7) | collective-permute-done | bytes 1048608 | tf_op jit(solution)/shard_map/ppermute | solution.py:47
  118.2 14.3 %all_to_all.26 = bf16[4,4,256,128]{3,2,1,0:T(8,128)(2,1)} all-to-all(bf16[4,4,256,128]{3,2,1,0:T(8,128)(2,1)S(1)} %add_convert_fusion), channel_id=1, replica_groups={{0,2,4,6},{16,18,20,22},{32,34,36,38},{48,50,52,54},{1,3,5,7},{17,19,21..., dimensions={0} | all-to-all | bytes 2097152 | tf_op jit(solution)/shard_map/all_to_all | solution.py:51
  134.0 14.5 %all_to_all.27 = bf16[16,64,128]{2,1,0:T(8,128)(2,1)} all-to-all(bf16[16,64,128]{2,1,0:T(8,128)(2,1)S(1)} %bitcast.23), channel_id=1, replica_groups=mesh['zh'=4,'x'=4,'core'=2,'y'=4,'zl'=2] {'zh','core','zl'}, dimensions={0} | all-to-all | bytes 524288 | tf_op jit(solution)/shard_map/all_to_all | solution.py:57
  149.5 11.0 %all_to_all.28 = bf16[8,2,64,128]{3,2,1,0:T(8,128)(2,1)S(1)} all-to-all(bf16[8,2,64,128]{3,2,1,0:T(8,128)(2,1)S(1)} %broadcast_in_dim.37), channel_id=1, replica_groups=mesh['zh'=4,'x'=4,'core'=2,'y'=4,'zl'=2] {'y','zl'}, dimensions={0} | all-to-all | bytes 524288 | tf_op jit(solution)/shard_map/all_to_all | solution.py:57
  160.6 6.5 %update.1 = (bf16[2,128,4096]{2,1,0:T(8,128)(2,1)}, f32[2,128,512]{2,1,0:T(8,128)}, f32[2,128,512]{2,1,0:T(8,128)}) custom-call(s32[1]{0:T(128)} %bitcast.pos, s32[2,2]{1,0:T(2,128)S(1)} %copy-done.4, bf16[4,2,2,64,128]{4,3,2,1,0:T(8,128)(2,1)S(1)} %bitcast.21, f32[2,128,512]{2,1,0:T(8,128)S(1)} %copy-done.2, f32[2,128,512]{2,1,0:T(8,128)S(1)} %copy-done.3, ...), custom_call_target="tpu_custom_call" | custom-call | tf_op jit(solution)/shard_map/update/pallas_call | solution.py:234
  (39 shorter events, 15.7 us)
Async XLA Ops:
  22.4 15.4 %all-to-all-start.1 = ((bf16[4,4,256,128]{3,2,1,0:T(8,128)(2,1)}), bf16[4,4,256,128]{3,2,1,0:T(8,128)(2,1)S(1)}, u32[]{:S(2)}, u32[]{:S(2)}) async-start(bf16[4,4,256,128]{3,2,1,0:T(8,128)(2,1)} %broadcast_in_dim.36), calls=%async_computation.1 | async-start | bytes 2097152 | tf_op jit(solution)/shard_map/all_to_all | solution.py:51
  37.8 14.8 %collective-permute-start.3 = (bf16[4,4,256,128]{3,2,1,0:T(8,128)(2,1)S(1)}, bf16[4,4,256,128]{3,2,1,0:T(8,128)(2,1)S(1)}, u32[]{:S(2)}, u32[]{:S(2)}) collective-permute-start(bf16[4,4,256,128]{3,2,1,0:T(8,128)(2,1)S(1)} %all-to-all-done.1.refs_0_), channel_id=1, source_target_pairs={{0,16},{16,32},{32,48},{48,0},{2,18},{18,34},{34,50},{50,2},{4,20}... | collective-permute-start | bytes 3145736 | tf_op jit(solution)/shard_map/ppermute | solution.py:47
  39.3 14.8 %collective-permute-start.4 = (bf16[4,4,256,128]{3,2,1,0:T(8,128)(2,1)S(1)}, bf16[4,4,256,128]{3,2,1,0:T(8,128)(2,1)S(1)}, u32[]{:S(2)}, u32[]{:S(2)}) collective-permute-start(bf16[4,4,256,128]{3,2,1,0:T(8,128)(2,1)S(1)} %all-to-all-done.1.refs_0_), channel_id=1, source_target_pairs={{0,48},{16,0},{32,16},{48,32},{2,50},{18,2},{34,18},{50,34},{4,52}... | collective-permute-start | bytes 3145736 | tf_op jit(solution)/shard_map/ppermute | solution.py:47
  39.8 26.2 %collective-permute-start.2 = (bf16[4,4,256,128]{3,2,1,0:T(8,128)(2,1)S(1)}, bf16[4,4,256,128]{3,2,1,0:T(8,128)(2,1)}, u32[]{:S(2)}, u32[]{:S(2)}) collective-permute-start(bf16[4,4,256,128]{3,2,1,0:T(8,128)(2,1)S(1)} %all-to-all-done.1.refs_0_), channel_id=1, source_target_pairs={{0,32},{16,48},{32,0},{48,16},{2,34},{18,50},{34,2},{50,18},{4,36}... | collective-permute-start | bytes 3145736 | tf_op jit(solution)/shard_map/ppermute | solution.py:47
  45.1 26.9 %collective-permute-start.1 = (bf16[256,4096]{1,0:T(8,128)(2,1)}, bf16[256,4096]{1,0:T(8,128)(2,1)}, u32[]{:S(2)}, u32[]{:S(2)}) collective-permute-start(bf16[256,4096]{1,0:T(8,128)(2,1)} %dynamic-slice_bitcast_fusion), channel_id=1, source_target_pairs={{0,8},{8,0},{1,9},{9,1},{2,10},{10,2},{3,11},{11,3},{4,12},{12,4},... | collective-permute-start | bytes 6291464 | tf_op jit(solution)/shard_map/ppermute | solution.py:65
  45.1 26.9 %collective-permute-start = (bf16[256,4096]{1,0:T(8,128)(2,1)}, bf16[256,4096]{1,0:T(8,128)(2,1)}, u32[]{:S(2)}, u32[]{:S(2)}) collective-permute-start(bf16[256,4096]{1,0:T(8,128)(2,1)} %a_near.1), channel_id=1, source_target_pairs={{0,8},{8,0},{1,9},{9,1},{2,10},{10,2},{3,11},{11,3},{4,12},{12,4},... | collective-permute-start | bytes 6291464 | tf_op jit(solution)/shard_map/ppermute | solution.py:65
  70.4 90.2 %collective-permute-start.8 = (bf16[4,128,4096]{2,1,0:T(8,128)(2,1)}, bf16[4,128,4096]{2,1,0:T(8,128)(2,1)}, u32[]{:S(2)}, u32[]{:S(2)}) collective-permute-start(bf16[4,128,4096]{2,1,0:T(8,128)(2,1)} %order.1.near_ref), channel_id=1, source_target_pairs={{0,8},{8,0},{1,9},{9,1},{2,10},{10,2},{3,11},{11,3},{4,12},{12,4},... | collective-permute-start | bytes 12582920 | tf_op jit(solution)/shard_map/ppermute | solution.py:65
  72.0 2.2 %copy-start = (bf16[2,256,4096]{2,1,0:T(8,128)(2,1)S(1)}, bf16[2,256,4096]{2,1,0:T(8,128)(2,1)}, u32[]{:S(2)}) copy-start(bf16[2,256,4096]{2,1,0:T(8,128)(2,1)} %c_near.1) | copy-start | bytes 12582916
  89.9 16.5 %collective-permute-start.5 = (bf16[4,4,256,128]{3,2,1,0:T(8,128)(2,1)S(1)}, bf16[4,4,256,128]{3,2,1,0:T(8,128)(2,1)S(1)}, u32[]{:S(2)}, u32[]{:S(2)}) collective-permute-start(bf16[4,4,256,128]{3,2,1,0:T(8,128)(2,1)S(1)} %grads.5), channel_id=1, source_target_pairs={{0,32},{16,48},{32,0},{48,16},{2,34},{18,50},{34,2},{50,18},{4,36}... | collective-permute-start | bytes 3145736 | tf_op jit(solution)/shard_map/ppermute | solution.py:47
  93.4 22.1 %collective-permute-start.6 = (bf16[4,4,256,128]{3,2,1,0:T(8,128)(2,1)S(1)}, bf16[4,4,256,128]{3,2,1,0:T(8,128)(2,1)S(1)}, u32[]{:S(2)}, u32[]{:S(2)}) collective-permute-start(bf16[4,4,256,128]{3,2,1,0:T(8,128)(2,1)S(1)} %grads.6), channel_id=1, source_target_pairs={{0,16},{16,32},{32,48},{48,0},{2,18},{18,34},{34,50},{50,2},{4,20}... | collective-permute-start | bytes 3145736 | tf_op jit(solution)/shard_map/ppermute | solution.py:47
  95.7 21.8 %collective-permute-start.7 = (bf16[4,4,256,128]{3,2,1,0:T(8,128)(2,1)S(1)}, bf16[4,4,256,128]{3,2,1,0:T(8,128)(2,1)S(1)}, u32[]{:S(2)}, u32[]{:S(2)}) collective-permute-start(bf16[4,4,256,128]{3,2,1,0:T(8,128)(2,1)S(1)} %grads.7), channel_id=1, source_target_pairs={{0,48},{16,0},{32,16},{48,32},{2,50},{18,2},{34,18},{50,34},{4,52}... | collective-permute-start | bytes 3145736 | tf_op jit(solution)/shard_map/ppermute | solution.py:47
  118.2 42.4 %copy-start.1 = (bf16[2,128,4096]{2,1,0:T(8,128)(2,1)S(1)}, bf16[2,128,4096]{2,1,0:T(8,128)(2,1)}, u32[]{:S(2)}) copy-start(bf16[2,128,4096]{2,1,0:T(8,128)(2,1)} %w_ref.1) | copy-start | bytes 6291460
  118.2 42.4 %copy-start.2 = (f32[2,128,512]{2,1,0:T(8,128)S(1)}, f32[2,128,512]{2,1,0:T(8,128)}, u32[]{:S(2)}) copy-start(f32[2,128,512]{2,1,0:T(8,128)} %m1_ref.1) | copy-start | bytes 1572868
  118.2 42.4 %copy-start.3 = (f32[2,128,512]{2,1,0:T(8,128)S(1)}, f32[2,128,512]{2,1,0:T(8,128)}, u32[]{:S(2)}) copy-start(f32[2,128,512]{2,1,0:T(8,128)} %m2_ref.1) | copy-start | bytes 1572868
  118.2 42.4 %copy-start.4 = (s32[2,2]{1,0:T(2,128)S(1)}, s32[2,2]{1,0:T(2,128)}, u32[]{:S(2)}) copy-start(s32[2,2]{1,0:T(2,128)} %settings.1) | copy-start | bytes 52

commit v3 on v2

v3 whole, which is shorter than its diff:
```python
import functools
import math

import jax
import jax.numpy as jnp
from jax import lax
from jax.experimental import pallas as pl
from jax.experimental.pallas import tpu as pltpu
from jax.sharding import Mesh, PartitionSpec as P


BETA_ONE = 0.9
BETA_TWO = 0.95
EPSILON = 1e-08
ZH, X, C, Y, ZL = SIZES = (4, 4, 2, 4, 2)
NAMES = ("zh", "x", "core", "y", "zl")
BF16 = jnp.bfloat16
F32 = jnp.float32
VMEM = pltpu.MemorySpace.VMEM
SMEM = pltpu.MemorySpace.SMEM
HBM = pltpu.MemorySpace.HBM


def mib(count):
    return pltpu.CompilerParams(vmem_limit_bytes=count << 20)


def flat_index(zh, x, c, y, zl):
    return (((zh * X + x) * C + c) * Y + y) * ZL + zl


def line_groups(axis_of_core):
    groups = []
    for c in range(C):
        for zh in range(ZH):
            for zl in range(ZL):
                for fixed in range(4):
                    if axis_of_core[c] == "x":
                        groups.append([flat_index(zh, i, c, fixed, zl) for i in range(X)])
                    else:
                        groups.append([flat_index(zh, fixed, c, i, zl) for i in range(Y)])
    return groups


WIDE = line_groups("xy")
NARROW = line_groups("yx")


def shift(v, groups, offset):
    pairs = [(g[i], g[(i + offset) % 4]) for g in groups for i in range(4)]
    return lax.ppermute(v, NAMES, pairs)


def swap_axes(v, axes):
    return lax.all_to_all(v, axes, split_axis=0, concat_axis=0, tiled=True)


def repeat(v, n):
    return jnp.broadcast_to(v[None], (n,) + v.shape)


def to_partner(v):
    return lax.ppermute(v, "core", [(0, 1), (1, 0)])


def place(core, a, b):
    first = core == 0
    return jnp.where(first, a, b), jnp.where(first, b, a)


def offset(position, shift_by):
    return (position + shift_by) & 3


def views(block, zh_from):
    if len(block.shape) == 4:
        return [(block, zh_from)]
    return [(block.at[h], zh_from + h * block.shape[2]) for h in range(block.shape[0])]


def coeffs_kernel(items, first, last, pos, x_ref, *refs):
    blocks, refs = refs[: len(items)], refs[len(items) :]
    acc = refs[-1]
    if first:
        acc[...] = jnp.zeros_like(acc)
    else:
        acc[...] = refs[0][...]
    for (a_off, b_offs, start), whole_block in zip(items, blocks):
        for i, b_off, (block, zh_from) in [
            (i, b_off, view)
            for view in views(whole_block, start)
            for i, b_off in enumerate(b_offs)
        ]:
            count = block.shape[1]
            x, y = place(pos[0], offset(pos[1], a_off), offset(pos[2], b_off))
            lhs = jnp.concatenate(
                [
                    x_ref[:, pl.ds(pl.multiple_of((zh * X + x) * 256, 256), 256)]
                    for zh in range(zh_from, zh_from + count)
                ],
                axis=1,
            )
            rhs = block[i].reshape(count * 256, 128)
            acc[y] += jnp.dot(lhs, rhs, preferred_element_type=F32)
    if last:
        refs[-2][...] = acc[...].astype(BF16)


def coeffs_step(pos, x, blocks, acc=None, last=False):
    shape = (4, x.shape[0], 128)
    items = tuple(block[1:] for block in blocks)
    ins = [pos, x, *(block[0] for block in blocks)] + ([] if acc is None else [acc])
    return pl.pallas_call(
        functools.partial(coeffs_kernel, items, acc is None, last),
        out_shape=jax.ShapeDtypeStruct(shape, BF16 if last else F32),
        in_specs=[pl.BlockSpec(memory_space=SMEM)]
        + [pl.BlockSpec(memory_space=VMEM)] * (len(ins) - 1),
        out_specs=pl.BlockSpec(memory_space=VMEM),
        scratch_shapes=[pltpu.VMEM(shape, F32)] if last else [],
        compiler_params=mib(14),
        name="coeffs",
    )(*ins)


def grad_kernel(items, pos, xt_ref, coeffs_ref, *out_refs):
    for (a_off, b_offs), out_ref in zip(items, out_refs):
        for i, b_off in enumerate(b_offs):
            x, y = place(pos[0], offset(pos[1], a_off), offset(pos[2], b_off))
            lhs = jnp.concatenate([xt_ref[zh, x] for zh in range(ZH)], axis=0)
            part = jnp.dot(lhs, coeffs_ref[y], preferred_element_type=F32)
            out_ref[i] = part.astype(BF16).reshape(ZH, 256, 128)


def grad_blocks(pos, xt, coeffs, *items):
    shapes = [
        jax.ShapeDtypeStruct((len(b_offs), ZH, 256, 128), BF16) for _, b_offs in items
    ]
    return pl.pallas_call(
        functools.partial(grad_kernel, items),
        out_shape=shapes,
        in_specs=[pl.BlockSpec(memory_space=SMEM)] + [pl.BlockSpec(memory_space=VMEM)] * 2,
        out_specs=[pl.BlockSpec(memory_space=VMEM)] * len(shapes),
        compiler_params=mib(12),
        name="grads",
    )(pos, xt, coeffs)


def order_kernel(items, pos, *refs):
    out_ref = refs[-1]
    for (a_off, b_offs, start), whole_block in zip(items, refs):
        for i, b_off, (block, zh_from) in [
            (i, b_off, view)
            for view in views(whole_block, start)
            for i, b_off in enumerate(b_offs)
        ]:
            x, y = place(pos[0], offset(pos[1], a_off), offset(pos[2], b_off))
            for j in range(block.shape[1]):
                lanes = pl.ds(pl.multiple_of(((zh_from + j) * X + x) * 256, 256), 256)
                out_ref[y, :, lanes] = block[i, j].T


def in_order(pos, blocks):
    return pl.pallas_call(
        functools.partial(order_kernel, tuple(block[1:] for block in blocks)),
        out_shape=jax.ShapeDtypeStruct((Y, 128, ZH * X * 256), BF16),
        in_specs=[pl.BlockSpec(memory_space=SMEM)]
        + [pl.BlockSpec(memory_space=VMEM)] * len(blocks),
        out_specs=pl.BlockSpec(memory_space=VMEM),
        compiler_params=mib(12),
        name="order",
    )(pos, *(block[0] for block in blocks))


def piece_kernel(pos, settings, p_ref, out_ref):
    mats, half, quarter = p_ref.shape
    column = lax.broadcasted_iota(jnp.int32, (half, quarter), 1) + pos[1] * quarter
    for k in range(mats):
        mine = jnp.where(column < settings[k, 0], p_ref[k].astype(F32), 0.0).astype(BF16)
        for zh in range(ZH):
            for zl in range(ZL):
                out_ref[zh, k, zl] = mine


def make_piece(pos, settings, projectors):
    mats, rows, rank_max = projectors.shape
    half, quarter = rows // ZL, rank_max // Y
    return pl.pallas_call(
        piece_kernel,
        out_shape=jax.ShapeDtypeStruct((ZH, mats, ZL, half, quarter), BF16),
        grid_spec=pltpu.PrefetchScalarGridSpec(
            num_scalar_prefetch=2,
            grid=(1,),
            in_specs=[
                pl.BlockSpec((mats, half, quarter), lambda i, pos, settings: (0, pos[0], pos[1]))
            ],
            out_specs=pl.BlockSpec(
                (ZH, mats, ZL, half, quarter), lambda i, pos, settings: (0, 0, 0, 0, 0)
            ),
        ),
        compiler_params=mib(4),
        name="piece",
    )(pos, settings, pltpu.with_memory_space_constraint(projectors, HBM))


def sides_kernel(pos, a_near, a_far, c_near, c_far, x_ref, xt_ref):
    tokens = a_near.shape[0]

    def write(projected, other):
        x_ref[:tokens, :] = projected[0]
        x_ref[tokens:, :] = projected[1]
        xt_ref[:, :tokens] = other[0].T
        xt_ref[:, tokens:] = other[1].T

    a = lambda: (a_near[...], a_far[...])
    c = lambda: (c_near[0], c_far[...])

    @pl.when(pos[1] == 0)
    def _():
        write(a(), c())

    @pl.when(pos[1] != 0)
    def _():
        write(c(), a())


def make_sides(pos, a_near, a_far, cotangents, c_far):
    tokens, features = a_near.shape
    chunk = 1024
    block = pl.BlockSpec((tokens, chunk), lambda j, pos: (0, j))
    return pl.pallas_call(
        sides_kernel,
        out_shape=(
            HBM((2 * tokens, features), BF16),
            HBM((features, 2 * tokens), BF16),
        ),
        grid_spec=pltpu.PrefetchScalarGridSpec(
            num_scalar_prefetch=1,
            grid=(features // chunk,),
            in_specs=[
                block,
                block,
                pl.BlockSpec((1, tokens, chunk), lambda j, pos: (pos[0], 0, j)),
                block,
            ],
            out_specs=(
                pl.BlockSpec((2 * tokens, chunk), lambda j, pos: (0, j)),
                pl.BlockSpec((chunk, 2 * tokens), lambda j, pos: (j, 0)),
            ),
        ),
        compiler_params=mib(20),
        name="sides",
    )(pos, *(pltpu.with_memory_space_constraint(v, HBM) for v in (a_near, a_far, cotangents, c_far)))


def update_kernel(
    scale, pos, settings, s_ref, m1_ref, m2_ref, near_ref, far_ref, w_ref,
    w_out, m1_out, m2_out, n_ref,
):
    mats = m1_ref.shape[0]
    half, quarter = s_ref.shape[3:]

    @pl.when(pl.program_id(0) == 0)
    def _():
        for k in range(mats):
            for y in range(Y):
                columns = slice(y * quarter, (y + 1) * quarter)
                column = lax.broadcasted_iota(jnp.int32, (half, quarter), 1) + y * quarter
                live = column < settings[k, 0]
                for z in range(ZL):
                    rows = slice(z * half, (z + 1) * half)
                    grad = s_ref[y, z, k].astype(F32) * scale
                    m1 = BETA_ONE * m1_ref[k, rows, columns] + (1.0 - BETA_ONE) * grad
                    m2 = BETA_TWO * m2_ref[k, rows, columns] + (1.0 - BETA_TWO) * grad * grad
                    m1 = jnp.where(live, m1, 0.0)
                    m2 = jnp.where(live, m2, 0.0)
                    m1_out[k, rows, columns] = m1
                    m2_out[k, rows, columns] = m2
                    normalized = jnp.where(live, m1 / (jnp.sqrt(m2) + EPSILON), 0.0)
                    n_ref[k, rows, columns] = normalized.astype(BF16)

    for k, p_ref in ((pos[0], near_ref), (1 - pos[0], far_ref)):
        rhs = p_ref[...].reshape(Y * quarter, p_ref.shape[2])
        update = jnp.dot(n_ref[k], rhs, preferred_element_type=F32)
        w_out[k] = (w_ref[k].astype(F32) - update).astype(BF16)


def apply_update(scale, pos, settings, s, m1, m2, near, far, weights):
    mats, rows, columns = weights.shape
    chunk = 2048

    def whole_block(shape):
        return pl.BlockSpec(shape, lambda j, *_: (0,) * len(shape))

    p_block = pl.BlockSpec((Y, near.shape[1], chunk), lambda j, *_: (0, 0, j))
    w_block = pl.BlockSpec((mats, rows, chunk), lambda j, *_: (0, 0, j))
    moments = whole_block(m1.shape)
    return pl.pallas_call(
        functools.partial(update_kernel, scale),
        out_shape=(
            jax.ShapeDtypeStruct(weights.shape, BF16),
            jax.ShapeDtypeStruct(m1.shape, F32),
            jax.ShapeDtypeStruct(m2.shape, F32),
        ),
        grid_spec=pltpu.PrefetchScalarGridSpec(
            num_scalar_prefetch=2,
            grid=(columns // chunk,),
            in_specs=[whole_block(s.shape), moments, moments, p_block, p_block, w_block],
            out_specs=(w_block, moments, moments),
            scratch_shapes=[pltpu.VMEM(m1.shape, BF16)],
        ),
        compiler_params=mib(24),
        name="update",
    )(pos, settings, s, m1, m2, near, far, weights)


def on_device(
    activations, cotangents, weights, projectors, first_moment, second_moment, matrix_settings
):
    mats, rows, rank_max = projectors.shape
    token_total = activations.shape[0] * 256
    grad_scale = 1.0 / math.sqrt(token_total)
    core = lax.axis_index("core")
    y = lax.axis_index("y")
    zl = lax.axis_index("zl")
    x = lax.axis_index("x")
    pos = jnp.stack([core, jnp.where(core == 0, x, y), jnp.where(core == 0, y, x)])
    pos = pos.astype(jnp.int32)
    live = jnp.arange(rank_max)[None, None, :] < matrix_settings[:, 0][:, None, None]
    half, quarter = rows // ZL, rank_max // Y

    far_index = 1 - core
    a_far = to_partner(activations)
    c_far = to_partner(lax.dynamic_index_in_dim(cotangents, far_index, 0, keepdims=False))

    piece = make_piece(jnp.stack([zl, y]).astype(jnp.int32), matrix_settings, projectors)
    g = swap_axes(piece.reshape(ZH * C * ZL, half, quarter), ("zh", "core", "zl"))
    g = g.reshape(ZH, 256, quarter)
    narrow, wide = {}, {}
    for o in (1, 3, 2):
        narrow[o] = shift(g, NARROW, o)
    for o in (1, 3, 2):
        wide[o] = shift(g, WIDE, o)
    rest = jnp.stack(
        [narrow[o].reshape(2, ZH // 2, 256, quarter) for o in (1, 3, 2)], axis=1
    )
    ahead = shift(rest, WIDE, 1)
    behind = shift(rest, WIDE, 3)
    low = shift(ahead[0], WIDE, 1)
    high = shift(behind[1], WIDE, 3)

    others = (-1, -3, -2)
    blocks_a = [(g[None], 0, (0,), 0)]
    blocks_a += [(narrow[o][None], 0, (-o,), 0) for o in (1, 3, 2)]
    blocks_a += [(wide[o][None], -o, (0,), 0) for o in (1, 3, 2)]
    blocks_b = [(ahead, -1, others, 0), (behind, -3, others, 0)]
    blocks_c = [(low, -2, others, 0), (high, -2, others, ZH // 2)]

    side = lax.dynamic_index_in_dim(matrix_settings[:, 1], core, 0, keepdims=False)
    projected_side, other_side = make_sides(
        jnp.stack([core, side]).astype(jnp.int32), activations, a_far, cotangents, c_far
    )
    other_side = other_side.reshape(ZH, X, 256, 512)

    acc = coeffs_step(pos, projected_side, blocks_a)
    acc = coeffs_step(pos, projected_side, blocks_b, acc)
    coeffs = coeffs_step(pos, projected_side, blocks_c, acc, last=True)

    away = (1, 2, 3)
    parts = []
    for o in (2, 1, 3):
        (block,) = grad_blocks(pos, other_side, coeffs, (o, away))
        parts.append(shift(block, WIDE, o))
    own_away, *home = grad_blocks(
        pos, other_side, coeffs, (0, away), *((o, (0,)) for o in (2, 1, 3, 0))
    )
    full = in_order(pos, blocks_a + blocks_b + blocks_c)
    full_far = to_partner(full)
    s = own_away.astype(F32)
    for part in parts:
        s = s + part.astype(F32)
    s = s.astype(BF16)
    total = home[3].astype(F32)
    narrows = []
    for i, o in enumerate(away):
        narrows.append(shift(s[i], NARROW, o))
    for i, o in enumerate((2, 1, 3)):
        total = total + shift(home[i], WIDE, o).astype(F32)
    for part in narrows:
        total = total + part.astype(F32)
    s = total.astype(BF16)
    s = swap_axes(s.reshape(ZH * C * ZL, half, quarter), ("zh", "core", "zl"))
    s = s.astype(F32).reshape(ZH, mats, ZL, half, quarter)
    s = jnp.sum(s, axis=(0, 2)).astype(BF16)
    s = swap_axes(repeat(s, Y * ZL), ("y", "zl"))
    return apply_update(
        grad_scale,
        pos,
        matrix_settings,
        s.reshape(Y, ZL, mats, half, quarter),
        first_moment,
        second_moment,
        full,
        full_far,
        weights,
    )


def solution(mesh):
    split = Mesh(mesh.devices.reshape(SIZES), NAMES)
    owner = ("zh", "x", "core")
    return jax.shard_map(
        on_device,
        mesh=split,
        in_specs=(
            P(NAMES, None),
            P(None, NAMES, None),
            P(None, owner, None),
            P(None, owner, None),
            P(None, owner, None),
            P(None, owner, None),
            P(),
        ),
        out_specs=(P(None, owner, None), P(None, owner, None), P(None, owner, None)),
        check_vma=False,
    )
```

time: 168 us -> 159 us (0.946)
  starting transfers between devices: 13 us -> 31 us
  waiting for transfers between devices: 49.6 us -> 31.8 us
  blocking collectives: 58.6 us -> 45.7 us
  local copies, waits for them, and re-layouts: 8.14 us -> 12.1 us
  other arithmetic: 5.01 us -> 1.67 us
  Pallas kernels: 31.9 us -> 33.7 us
    ppermute x6 -> x19, starting transfers between devices: 7.99 us -> 30.5 us  [shift(): return lax.ppermute(v, NAMES, pairs)]
    all_to_all x1 -> x0, blocking collectives: 14.3 us -> none  [swap_lines(): lax.all_to_all(v, NAMES, split_axis=0, concat_axis=0, tiled=True, axis_in...]
    all_to_all x1 -> x0, waiting for transfers between devices: 10.9 us -> none  [swap_lines(): lax.all_to_all(v, NAMES, split_axis=0, concat_axis=0, tiled=True, axis_in...]
    ppermute x6 -> x19, waiting for transfers between devices: 38.7 us -> 31.8 us  [shift(): return lax.ppermute(v, NAMES, pairs)]
    unnamed x10 -> x26, local copies, waits for them, and re-layouts: 2.21 us -> 6.69 us
    all_to_all x1 -> x0, starting transfers between devices: 4.46 us -> none  [swap_lines(): lax.all_to_all(v, NAMES, split_axis=0, concat_axis=0, tiled=True, axis_in...]
    pallas_call x9 -> x10, Pallas kernels: 25.4 us -> 27.9 us  [the longest x1 8.06 us: make_sides(): pl.pallas_call(sides_kernel, out_shape=(HBM((2 * tokens, features), BF16)...]
  transfers between devices with their start and end apart: 10 -> 22, of which waited for: 7 -> 12; matrix products, arithmetic and copies ran while one was open for 5% -> 4% of each run, Pallas kernels for 15% -> 17%
where the time goes in v3:
time: 159 us; the launch traced here: 157 us
  blocking collectives  45.7 us (29%)
  Pallas kernels  33.7 us (21%)
  waiting for transfers between devices  31.8 us (20%)
  starting transfers between devices  31 us (19%)
  local copies, waits for them, and re-layouts  12.1 us (8%)
  other arithmetic  1.67 us (1%)
    all_to_all x3, blocking collectives, swap_axes(): return lax.all_to_all(v, axes, split_axis=0, concat_axis=0, tiled=True)  45.7 us
    ppermute x19, waiting for transfers between devices, shift(): return lax.ppermute(v, NAMES, pairs)  31.8 us
    ppermute x19, starting transfers between devices, shift(): return lax.ppermute(v, NAMES, pairs)  30.5 us
    pallas_call x1, Pallas kernels, make_sides(): pl.pallas_call(sides_kernel, out_shape=(HBM((2 * tokens, features), BF16)...  8.06 us
    pallas_call x3, Pallas kernels, coeffs_step(): pl.pallas_call(functools.partial(coeffs_kernel, items, acc is None, last)...  7.26 us
    pallas_call x4, Pallas kernels, grad_blocks(): pl.pallas_call(functools.partial(grad_kernel, items), out_shape=shapes, i...  7.18 us
    unnamed x26, local copies, waits for them, and re-layouts  6.69 us
    pallas_call x1, Pallas kernels, apply_update(): pl.pallas_call(functools.partial(update_kernel, scale), out_shape=(jax.Sh...  5.78 us
  transfers between devices with their start and end apart: 22, of which 12 were waited for; matrix products, arithmetic and copies ran while one was open for 4% of the time, Pallas kernels for 17%

profile of v3, /device:TPU:2, one launch (start us, length us, event | category | flops | bytes accessed | tf_op | source)
XLA Modules:
  0.0 156.7 jit_solution(5203344956272305071)
XLA Ops:
  2.7 18.8 %all_to_all.15 = bf16[16,64,128]{2,1,0:T(8,128)(2,1)S(1)} all-to-all(bf16[16,64,128]{2,1,0:T(8,128)(2,1)S(1)} %bitcast.69), channel_id=1, replica_groups=mesh['zh'=4,'x'=4,'core'=2,'y'=4,'zl'=2] {'zh','core','zl'}, dimensions={0} | all-to-all | bytes 524288 | tf_op jit(solution)/shard_map/all_to_all | solution.py:55
  24.7 2.0 %collective-permute-start.4 = (bf16[4,256,128]{2,1,0:T(8,128)(2,1)S(1)}, bf16[4,256,128]{2,1,0:T(8,128)(2,1)S(1)}, u32[]{:S(2)}, u32[]{:S(2)}) collective-permute-start(bf16[4,256,128]{2,1,0:T(8,128)(2,1)S(1)} %bitcast.49), channel_id=1, source_target_pairs={{0,4},{2,6},{4,0},{6,2},{16,20},{18,22},{20,16},{22,18},{32,36},{3... | collective-permute-start | bytes 786440 | tf_op jit(solution)/shard_map/ppermute | solution.py:51
  26.7 2.4 %collective-permute-done.2 = bf16[4,256,128]{2,1,0:T(8,128)(2,1)S(1)} collective-permute-done((bf16[4,256,128]{2,1,0:T(8,128)(2,1)S(1)}, bf16[4,256,128]{2,1,0:T(8,128)(2,1)S(1)}, u32[]{:S(2)}, u32[]{:S(2)}) %collective-permute-start.2) | collective-permute-done | bytes 262176 | tf_op jit(solution)/shard_map/ppermute | solution.py:51
  29.4 3.7 %collective-permute-done.4 = bf16[4,256,128]{2,1,0:T(8,128)(2,1)S(1)} collective-permute-done((bf16[4,256,128]{2,1,0:T(8,128)(2,1)S(1)}, bf16[4,256,128]{2,1,0:T(8,128)(2,1)S(1)}, u32[]{:S(2)}, u32[]{:S(2)}) %collective-permute-start.4) | collective-permute-done | bytes 262176 | tf_op jit(solution)/shard_map/ppermute | solution.py:51
  35.3 3.1 %dynamic-slice_bitcast_fusion = bf16[256,4096]{1,0:T(8,128)(2,1)} fusion(bf16[2,256,4096]{2,1,0:T(8,128)(2,1)} %c_near.1, s32[]{:T(128)S(6)} %select_n.18), kind=kLoop, calls=%fused_computation | loop fusion | bytes 4194308 | tf_op jit(solution)/shard_map/jit(dynamic_index_in_dim)/squeeze | solution.py:333
  40.5 4.8 %collective-permute-done.5.refs_0_.refs_7_ = bf16[2,3,2,256,128]{4,3,2,1,0:T(8,128)(2,1)S(1)} collective-permute-done((bf16[2,3,2,256,128]{4,3,2,1,0:T(8,128)(2,1)S(1)}, bf16[2,3,2,256,128]{4,3,2,1,0:T(8,128)(2,1)S(1)}, u32[]{:S(2)}, u32[]{:S(2)}) %collective-permute-start.5) | collective-permute-done | bytes 786464 | tf_op jit(solution)/shard_map/ppermute | solution.py:51
  52.4 3.3 %collective-permute-start.11 = (bf16[4,256,128]{2,1,0:T(8,128)(2,1)S(1)}, bf16[4,256,128]{2,1,0:T(8,128)(2,1)}, u32[]{:S(2)}, u32[]{:S(2)}) collective-permute-start(bf16[4,256,128]{2,1,0:T(8,128)(2,1)S(1)} %bitcast.52), channel_id=1, source_target_pairs={{0,32},{16,48},{32,0},{48,16},{2,34},{18,50},{34,2},{50,18},{4,36}... | collective-permute-start | bytes 786440 | tf_op jit(solution)/shard_map/ppermute | solution.py:51
  55.8 6.0 %collective-permute-done.11 = bf16[4,256,128]{2,1,0:T(8,128)(2,1)} collective-permute-done((bf16[4,256,128]{2,1,0:T(8,128)(2,1)S(1)}, bf16[4,256,128]{2,1,0:T(8,128)(2,1)}, u32[]{:S(2)}, u32[]{:S(2)}) %collective-permute-start.11) | collective-permute-done | bytes 262176 | tf_op jit(solution)/shard_map/ppermute | solution.py:51
  63.7 4.1 %order.1.near_ref = bf16[4,128,4096]{2,1,0:T(8,128)(2,1)} custom-call(s32[3]{0:T(128)S(1)} %pad_add_fusion.pos, bf16[1,4,256,128]{3,2,1,0:T(8,128)(2,1)S(1)} %bitcast.53, bf16[1,4,256,128]{3,2,1,0:T(8,128)(2,1)S(1)} %bitcast.56, bf16[1,4,256,128]{3,2,1,0:T(8,128)(2,1)S(1)} %bitcast.59, bf16[1,4,256,128]{3,2,1,0:T(8,128)(2,1)S(1)} %bitcast.62, ...), custom_call_target="tpu_custom_call" | custom-call | tf_op jit(solution)/shard_map/order/pallas_call | solution.py:163
  69.1 8.1 %sides.1 = (bf16[512,4096]{1,0:T(8,128)(2,1)}, bf16[4096,512]{1,0:T(8,128)(2,1)}) custom-call(s32[2]{0:T(128)S(1)} %pad_add_fusion.1.pos, bf16[256,4096]{1,0:T(8,128)(2,1)} %a_near.1, bf16[256,4096]{1,0:T(8,128)(2,1)} %collective-permute-done.a_far, bf16[2,256,4096]{2,1,0:T(8,128)(2,1)} %c_near.1, bf16[256,4096]{1,0:T(8,128)(2,1)} %collective-permute-done.1.c_far), custom_call_target="tpu_custom_call" | custom-call | tf_op jit(solution)/shard_map/sides/pallas_call | solution.py:230
  77.2 2.2 %copy-done.1 = bf16[512,4096]{1,0:T(8,128)(2,1)S(1)} copy-done((bf16[512,4096]{1,0:T(8,128)(2,1)S(1)}, bf16[512,4096]{1,0:T(8,128)(2,1)}, u32[]{:S(2)}) %copy-start.1) | copy-done | bytes 4194328
  79.4 3.1 %coeffs.3.refs_2_ = f32[4,512,128]{2,1,0:T(8,128)S(1)} custom-call(s32[3]{0:T(128)S(1)} %pad_add_fusion.pos, bf16[512,4096]{1,0:T(8,128)(2,1)S(1)} %copy-done.1, bf16[1,4,256,128]{3,2,1,0:T(8,128)(2,1)S(1)} %bitcast.54, bf16[1,4,256,128]{3,2,1,0:T(8,128)(2,1)S(1)} %bitcast.57, bf16[1,4,256,128]{3,2,1,0:T(8,128)(2,1)S(1)} %bitcast.60, ...), custom_call_target="tpu_custom_call" | custom-call | tf_op jit(solution)/shard_map/coeffs/pallas_call | solution.py:113
  82.5 2.4 %coeffs.4.refs_2_ = f32[4,512,128]{2,1,0:T(8,128)S(1)} custom-call(s32[3]{0:T(128)S(1)} %pad_add_fusion.pos, bf16[512,4096]{1,0:T(8,128)(2,1)S(1)} %copy-done.1, bf16[2,3,2,256,128]{4,3,2,1,0:T(8,128)(2,1)S(1)} %collective-permute-done.5.refs_0_.refs_7_, bf16[2,3,2,256,128]{4,3,2,1,0:T(8,128)(2,1)S(1)} %collective-permute-done.7.refs_1_.refs_8_, ...), custom_call_target="tpu_custom_call" | custom-call | tf_op jit(solution)/shard_map/coeffs/pallas_call | solution.py:113
  88.7 3.2 %collective-permute-start.15 = (bf16[3,4,256,128]{3,2,1,0:T(8,128)(2,1)S(1)}, bf16[3,4,256,128]{3,2,1,0:T(8,128)(2,1)S(1)}, u32[]{:S(2)}, u32[]{:S(2)}) collective-permute-start(bf16[3,4,256,128]{3,2,1,0:T(8,128)(2,1)S(1)} %grads.5), channel_id=1, source_target_pairs={{0,32},{16,48},{32,0},{48,16},{2,34},{18,50},{34,2},{50,18},{4,36}... | collective-permute-start | bytes 2359304 | tf_op jit(solution)/shard_map/ppermute | solution.py:51
  95.1 2.1 %collective-permute-start.17 = (bf16[3,4,256,128]{3,2,1,0:T(8,128)(2,1)S(1)}, bf16[3,4,256,128]{3,2,1,0:T(8,128)(2,1)S(1)}, u32[]{:S(2)}, u32[]{:S(2)}) collective-permute-start(bf16[3,4,256,128]{3,2,1,0:T(8,128)(2,1)S(1)} %grads.7), channel_id=1, source_target_pairs={{0,48},{16,0},{32,16},{48,32},{2,50},{18,2},{34,18},{50,34},{4,52}... | collective-permute-start | bytes 2359304 | tf_op jit(solution)/shard_map/ppermute | solution.py:51
  97.2 2.6 %grads.4 = (bf16[3,4,256,128]{3,2,1,0:T(8,128)(2,1)S(1)}, bf16[1,4,256,128]{3,2,1,0:T(8,128)(2,1)S(1)}, bf16[1,4,256,128]{3,2,1,0:T(8,128)(2,1)S(1)}, bf16[1,4,2...) custom-call(s32[3]{0:T(128)S(1)} %pad_add_fusion.pos, bf16[4,4,256,512]{3,2,1,0:T(8,128)(2,1)S(1)} %bitcast.46, ...), custom_call_target="tpu_custom_call" | custom-call | tf_op jit(solution)/shard_map/grads/pallas_call | solution.py:138
  102.4 6.9 %collective-permute-done.16 = bf16[3,4,256,128]{3,2,1,0:T(8,128)(2,1)S(1)} collective-permute-done((bf16[3,4,256,128]{3,2,1,0:T(8,128)(2,1)S(1)}, bf16[3,4,256,128]{3,2,1,0:T(8,128)(2,1)S(1)}, u32[]{:S(2)}, u32[]{:S(2)}) %collective-permute-start.16) | collective-permute-done | bytes 786464 | tf_op jit(solution)/shard_map/ppermute | solution.py:51
  109.3 2.3 %collective-permute-start.14 = (bf16[1,4,256,128]{3,2,1,0:T(8,128)(2,1)S(1)}, bf16[1,4,256,128]{3,2,1,0:T(8,128)(2,1)S(1)}, u32[]{:S(2)}, u32[]{:S(2)}) collective-permute-start(bf16[1,4,256,128]{3,2,1,0:T(8,128)(2,1)S(1)} %get-tuple-element.15), channel_id=1, source_target_pairs={{0,48},{16,0},{32,16},{48,32},{2,50},{18,2},{34,18},{50,34},{4,52}... | collective-permute-start | bytes 786440 | tf_op jit(solution)/shard_map/ppermute | solution.py:51
  113.7 2.0 %collective-permute-start.19 = (bf16[4,256,128]{2,1,0:T(8,128)(2,1)S(1)}, bf16[4,256,128]{2,1,0:T(8,128)(2,1)S(1)}, u32[]{:S(2)}, u32[]{:S(2)}) collective-permute-start(bf16[4,256,128]{2,1,0:T(8,128)(2,1)S(1)} %get-tuple-element.19), channel_id=1, source_target_pairs={{0,4},{2,6},{4,0},{6,2},{16,20},{18,22},{20,16},{22,18},{32,36},{3... | collective-permute-start | bytes 786440 | tf_op jit(solution)/shard_map/ppermute | solution.py:51
  116.0 2.6 %collective-permute-start.20 = (bf16[4,256,128]{2,1,0:T(8,128)(2,1)S(1)}, bf16[4,256,128]{2,1,0:T(8,128)(2,1)S(1)}, u32[]{:S(2)}, u32[]{:S(2)}) collective-permute-start(bf16[4,256,128]{2,1,0:T(8,128)(2,1)S(1)} %get-tuple-element.18), channel_id=1, source_target_pairs={{0,6},{2,0},{4,2},{6,4},{16,22},{18,16},{20,18},{22,20},{32,38},{3... | collective-permute-start | bytes 786440 | tf_op jit(solution)/shard_map/ppermute | solution.py:51
  119.8 3.0 %collective-permute-done.19 = bf16[4,256,128]{2,1,0:T(8,128)(2,1)S(1)} collective-permute-done((bf16[4,256,128]{2,1,0:T(8,128)(2,1)S(1)}, bf16[4,256,128]{2,1,0:T(8,128)(2,1)S(1)}, u32[]{:S(2)}, u32[]{:S(2)}) %collective-permute-start.19) | collective-permute-done | bytes 262176 | tf_op jit(solution)/shard_map/ppermute | solution.py:51
  123.9 14.4 %all_to_all.16 = bf16[16,64,128]{2,1,0:T(8,128)(2,1)S(1)} all-to-all(bf16[16,64,128]{2,1,0:T(8,128)(2,1)S(1)} %bitcast.71), channel_id=1, replica_groups=mesh['zh'=4,'x'=4,'core'=2,'y'=4,'zl'=2] {'zh','core','zl'}, dimensions={0} | all-to-all | bytes 524288 | tf_op jit(solution)/shard_map/all_to_all | solution.py:55
  138.3 12.6 %all_to_all.17 = bf16[8,2,64,128]{3,2,1,0:T(8,128)(2,1)S(1)} all-to-all(bf16[8,2,64,128]{3,2,1,0:T(8,128)(2,1)S(1)} %broadcast_in_dim.54), channel_id=1, replica_groups=mesh['zh'=4,'x'=4,'core'=2,'y'=4,'zl'=2] {'y','zl'}, dimensions={0} | all-to-all | bytes 524288 | tf_op jit(solution)/shard_map/all_to_all | solution.py:55
  150.9 5.8 %update.1 = (bf16[2,128,4096]{2,1,0:T(8,128)(2,1)}, f32[2,128,512]{2,1,0:T(8,128)}, f32[2,128,512]{2,1,0:T(8,128)}) custom-call(s32[3]{0:T(128)S(1)} %pad_add_fusion.pos, s32[2,2]{1,0:T(2,128)S(1)} %copy-done.12, bf16[4,2,2,64,128]{4,3,2,1,0:T(8,128)(2,1)S(1)} %bitcast.68, f32[2,128,512]{2,1,0:T(8,128)S(1)} %copy-done.9, f32[2,128,512]{2,1,0:T(8,128)S(1)} %copy-done.10, ...), custom_call_target="tpu_custom_call" | custom-call | tf_op jit(solution)/shard_map/update/pallas_call | solution.py:297
  (74 shorter events, 34.3 us)
Async XLA Ops:
  21.5 7.6 %collective-permute-start.2 = (bf16[4,256,128]{2,1,0:T(8,128)(2,1)S(1)}, bf16[4,256,128]{2,1,0:T(8,128)(2,1)S(1)}, u32[]{:S(2)}, u32[]{:S(2)}) collective-permute-start(bf16[4,256,128]{2,1,0:T(8,128)(2,1)S(1)} %bitcast.47), channel_id=1, source_target_pairs={{0,2},{2,4},{4,6},{6,0},{16,18},{18,20},{20,22},{22,16},{32,34},{3... | collective-permute-start | bytes 786440 | tf_op jit(solution)/shard_map/ppermute | solution.py:51
  23.1 6.4 %collective-permute-start.3 = (bf16[4,256,128]{2,1,0:T(8,128)(2,1)S(1)}, bf16[4,256,128]{2,1,0:T(8,128)(2,1)S(1)}, u32[]{:S(2)}, u32[]{:S(2)}) collective-permute-start(bf16[4,256,128]{2,1,0:T(8,128)(2,1)S(1)} %bitcast.48), channel_id=1, source_target_pairs={{0,6},{2,0},{4,2},{6,4},{16,22},{18,16},{20,18},{22,20},{32,38},{3... | collective-permute-start | bytes 786440 | tf_op jit(solution)/shard_map/ppermute | solution.py:51
  24.7 8.4 %collective-permute-start.4 = (bf16[4,256,128]{2,1,0:T(8,128)(2,1)S(1)}, bf16[4,256,128]{2,1,0:T(8,128)(2,1)S(1)}, u32[]{:S(2)}, u32[]{:S(2)}) collective-permute-start(bf16[4,256,128]{2,1,0:T(8,128)(2,1)S(1)} %bitcast.49), channel_id=1, source_target_pairs={{0,4},{2,6},{4,0},{6,2},{16,20},{18,22},{20,16},{22,18},{32,36},{3... | collective-permute-start | bytes 786440 | tf_op jit(solution)/shard_map/ppermute | solution.py:51
  33.2 12.1 %collective-permute-start.5 = (bf16[2,3,2,256,128]{4,3,2,1,0:T(8,128)(2,1)S(1)}, bf16[2,3,2,256,128]{4,3,2,1,0:T(8,128)(2,1)S(1)}, u32[]{:S(2)}, u32[]{:S(2)}) collective-permute-start(bf16[2,3,2,256,128]{4,3,2,1,0:T(8,128)(2,1)S(1)} %pad_maximum_fusion), channel_id=1, source_target_pairs={{0,16},{16,32},{32,48},{48,0},{2,18},{18,34},{34,50},{50,2},{4,20}... | collective-permute-start | bytes 2359304 | tf_op jit(solution)/shard_map/ppermute | solution.py:51
  34.8 13.0 %collective-permute-start.7 = (bf16[2,3,2,256,128]{4,3,2,1,0:T(8,128)(2,1)S(1)}, bf16[2,3,2,256,128]{4,3,2,1,0:T(8,128)(2,1)S(1)}, u32[]{:S(2)}, u32[]{:S(2)}) collective-permute-start(bf16[2,3,2,256,128]{4,3,2,1,0:T(8,128)(2,1)S(1)} %pad_maximum_fusion), channel_id=1, source_target_pairs={{0,48},{16,0},{32,16},{48,32},{2,50},{18,2},{34,18},{50,34},{4,52}... | collective-permute-start | bytes 2359304 | tf_op jit(solution)/shard_map/ppermute | solution.py:51
  38.5 30.6 %collective-permute-start.1 = (bf16[256,4096]{1,0:T(8,128)(2,1)}, bf16[256,4096]{1,0:T(8,128)(2,1)}, u32[]{:S(2)}, u32[]{:S(2)}) collective-permute-start(bf16[256,4096]{1,0:T(8,128)(2,1)} %dynamic-slice_bitcast_fusion), channel_id=1, source_target_pairs={{0,8},{8,0},{1,9},{9,1},{2,10},{10,2},{3,11},{11,3},{4,12},{12,4},... | collective-permute-start | bytes 6291464 | tf_op jit(solution)/shard_map/ppermute | solution.py:63
  38.5 30.6 %collective-permute-start = (bf16[256,4096]{1,0:T(8,128)(2,1)}, bf16[256,4096]{1,0:T(8,128)(2,1)}, u32[]{:S(2)}, u32[]{:S(2)}) collective-permute-start(bf16[256,4096]{1,0:T(8,128)(2,1)} %a_near.1), channel_id=1, source_target_pairs={{0,8},{8,0},{1,9},{9,1},{2,10},{10,2},{3,11},{11,3},{4,12},{12,4},... | collective-permute-start | bytes 6291464 | tf_op jit(solution)/shard_map/ppermute | solution.py:63
  39.0 9.9 %collective-permute-start.9 = (bf16[4,256,128]{2,1,0:T(8,128)(2,1)S(1)}, bf16[4,256,128]{2,1,0:T(8,128)(2,1)S(1)}, u32[]{:S(2)}, u32[]{:S(2)}) collective-permute-start(bf16[4,256,128]{2,1,0:T(8,128)(2,1)S(1)} %bitcast.50), channel_id=1, source_target_pairs={{0,16},{16,32},{32,48},{48,0},{2,18},{18,34},{34,50},{50,2},{4,20}... | collective-permute-start | bytes 786440 | tf_op jit(solution)/shard_map/ppermute | solution.py:51
  45.3 6.4 %collective-permute-start.10 = (bf16[4,256,128]{2,1,0:T(8,128)(2,1)S(1)}, bf16[4,256,128]{2,1,0:T(8,128)(2,1)S(1)}, u32[]{:S(2)}, u32[]{:S(2)}) collective-permute-start(bf16[4,256,128]{2,1,0:T(8,128)(2,1)S(1)} %bitcast.51), channel_id=1, source_target_pairs={{0,48},{16,0},{32,16},{48,32},{2,50},{18,2},{34,18},{50,34},{4,52}... | collective-permute-start | bytes 786440 | tf_op jit(solution)/shard_map/ppermute | solution.py:51
  47.8 14.0 %collective-permute-start.6 = (bf16[3,2,256,128]{3,2,1,0:T(8,128)(2,1)}, bf16[3,2,256,128]{3,2,1,0:T(8,128)(2,1)S(1)}, u32[]{:S(2)}, u32[]{:S(2)}) collective-permute-start(bf16[3,2,256,128]{3,2,1,0:T(8,128)(2,1)} %slice_bitcast_fusion.1), channel_id=1, source_target_pairs={{0,16},{16,32},{32,48},{48,0},{2,18},{18,34},{34,50},{50,2},{4,20}... | collective-permute-start | bytes 1179656 | tf_op jit(solution)/shard_map/ppermute | solution.py:51
  49.6 12.2 %collective-permute-start.8 = (bf16[3,2,256,128]{3,2,1,0:T(8,128)(2,1)}, bf16[3,2,256,128]{3,2,1,0:T(8,128)(2,1)S(1)}, u32[]{:S(2)}, u32[]{:S(2)}) collective-permute-start(bf16[3,2,256,128]{3,2,1,0:T(8,128)(2,1)} %slice_bitcast_fusion), channel_id=1, source_target_pairs={{0,48},{16,0},{32,16},{48,32},{2,50},{18,2},{34,18},{50,34},{4,52}... | collective-permute-start | bytes 1179656 | tf_op jit(solution)/shard_map/ppermute | solution.py:51
  52.4 9.4 %collective-permute-start.11 = (bf16[4,256,128]{2,1,0:T(8,128)(2,1)S(1)}, bf16[4,256,128]{2,1,0:T(8,128)(2,1)}, u32[]{:S(2)}, u32[]{:S(2)}) collective-permute-start(bf16[4,256,128]{2,1,0:T(8,128)(2,1)S(1)} %bitcast.52), channel_id=1, source_target_pairs={{0,32},{16,48},{32,0},{48,16},{2,34},{18,50},{34,2},{50,18},{4,36}... | collective-permute-start | bytes 786440 | tf_op jit(solution)/shard_map/ppermute | solution.py:51
  67.8 83.2 %collective-permute-start.21 = (bf16[4,128,4096]{2,1,0:T(8,128)(2,1)}, bf16[4,128,4096]{2,1,0:T(8,128)(2,1)}, u32[]{:S(2)}, u32[]{:S(2)}) collective-permute-start(bf16[4,128,4096]{2,1,0:T(8,128)(2,1)} %order.1.near_ref), channel_id=1, source_target_pairs={{0,8},{8,0},{1,9},{9,1},{2,10},{10,2},{3,11},{11,3},{4,12},{12,4},... | collective-permute-start | bytes 12582920 | tf_op jit(solution)/shard_map/ppermute | solution.py:63
  88.7 13.7 %collective-permute-start.15 = (bf16[3,4,256,128]{3,2,1,0:T(8,128)(2,1)S(1)}, bf16[3,4,256,128]{3,2,1,0:T(8,128)(2,1)S(1)}, u32[]{:S(2)}, u32[]{:S(2)}) collective-permute-start(bf16[3,4,256,128]{3,2,1,0:T(8,128)(2,1)S(1)} %grads.5), channel_id=1, source_target_pairs={{0,32},{16,48},{32,0},{48,16},{2,34},{18,50},{34,2},{50,18},{4,36}... | collective-permute-start | bytes 2359304 | tf_op jit(solution)/shard_map/ppermute | solution.py:51
  93.4 15.8 %collective-permute-start.16 = (bf16[3,4,256,128]{3,2,1,0:T(8,128)(2,1)S(1)}, bf16[3,4,256,128]{3,2,1,0:T(8,128)(2,1)S(1)}, u32[]{:S(2)}, u32[]{:S(2)}) collective-permute-start(bf16[3,4,256,128]{3,2,1,0:T(8,128)(2,1)S(1)} %grads.6), channel_id=1, source_target_pairs={{0,16},{16,32},{32,48},{48,0},{2,18},{18,34},{34,50},{50,2},{4,20}... | collective-permute-start | bytes 2359304 | tf_op jit(solution)/shard_map/ppermute | solution.py:51
  95.1 16.6 %collective-permute-start.17 = (bf16[3,4,256,128]{3,2,1,0:T(8,128)(2,1)S(1)}, bf16[3,4,256,128]{3,2,1,0:T(8,128)(2,1)S(1)}, u32[]{:S(2)}, u32[]{:S(2)}) collective-permute-start(bf16[3,4,256,128]{3,2,1,0:T(8,128)(2,1)S(1)} %grads.7), channel_id=1, source_target_pairs={{0,48},{16,0},{32,16},{48,32},{2,50},{18,2},{34,18},{50,34},{4,52}... | collective-permute-start | bytes 2359304 | tf_op jit(solution)/shard_map/ppermute | solution.py:51
  99.8 13.9 %collective-permute-start.12 = (bf16[1,4,256,128]{3,2,1,0:T(8,128)(2,1)S(1)}, bf16[1,4,256,128]{3,2,1,0:T(8,128)(2,1)S(1)}, u32[]{:S(2)}, u32[]{:S(2)}) collective-permute-start(bf16[1,4,256,128]{3,2,1,0:T(8,128)(2,1)S(1)} %get-tuple-element.13), channel_id=1, source_target_pairs={{0,32},{16,48},{32,0},{48,16},{2,34},{18,50},{34,2},{50,18},{4,36}... | collective-permute-start | bytes 786440 | tf_op jit(solution)/shard_map/ppermute | solution.py:51
  102.4 13.7 %collective-permute-start.13 = (bf16[1,4,256,128]{3,2,1,0:T(8,128)(2,1)S(1)}, bf16[1,4,256,128]{3,2,1,0:T(8,128)(2,1)S(1)}, u32[]{:S(2)}, u32[]{:S(2)}) collective-permute-start(bf16[1,4,256,128]{3,2,1,0:T(8,128)(2,1)S(1)} %get-tuple-element.14), channel_id=1, source_target_pairs={{0,16},{16,32},{32,48},{48,0},{2,18},{18,34},{34,50},{50,2},{4,20}... | collective-permute-start | bytes 786440 | tf_op jit(solution)/shard_map/ppermute | solution.py:51
  109.3 9.4 %collective-permute-start.14 = (bf16[1,4,256,128]{3,2,1,0:T(8,128)(2,1)S(1)}, bf16[1,4,256,128]{3,2,1,0:T(8,128)(2,1)S(1)}, u32[]{:S(2)}, u32[]{:S(2)}) collective-permute-start(bf16[1,4,256,128]{3,2,1,0:T(8,128)(2,1)S(1)} %get-tuple-element.15), channel_id=1, source_target_pairs={{0,48},{16,0},{32,16},{48,32},{2,50},{18,2},{34,18},{50,34},{4,52}... | collective-permute-start | bytes 786440 | tf_op jit(solution)/shard_map/ppermute | solution.py:51
  112.1 38.8 %copy-start.2 = (bf16[2,128,4096]{2,1,0:T(8,128)(2,1)S(1)}, bf16[2,128,4096]{2,1,0:T(8,128)(2,1)}, u32[]{:S(2)}) copy-start(bf16[2,128,4096]{2,1,0:T(8,128)(2,1)} %w_ref.1) | copy-start | bytes 6291460
  112.1 38.8 %copy-start.9 = (f32[2,128,512]{2,1,0:T(8,128)S(1)}, f32[2,128,512]{2,1,0:T(8,128)}, u32[]{:S(2)}) copy-start(f32[2,128,512]{2,1,0:T(8,128)} %m1_ref.1) | copy-start | bytes 1572868
  112.2 7.7 %collective-permute-start.18 = (bf16[4,256,128]{2,1,0:T(8,128)(2,1)S(1)}, bf16[4,256,128]{2,1,0:T(8,128)(2,1)S(1)}, u32[]{:S(2)}, u32[]{:S(2)}) collective-permute-start(bf16[4,256,128]{2,1,0:T(8,128)(2,1)S(1)} %get-tuple-element.17), channel_id=1, source_target_pairs={{0,2},{2,4},{4,6},{6,0},{16,18},{18,20},{20,22},{22,16},{32,34},{3... | collective-permute-start | bytes 786440 | tf_op jit(solution)/shard_map/ppermute | solution.py:51
  113.7 9.2 %collective-permute-start.19 = (bf16[4,256,128]{2,1,0:T(8,128)(2,1)S(1)}, bf16[4,256,128]{2,1,0:T(8,128)(2,1)S(1)}, u32[]{:S(2)}, u32[]{:S(2)}) collective-permute-start(bf16[4,256,128]{2,1,0:T(8,128)(2,1)S(1)} %get-tuple-element.19), channel_id=1, source_target_pairs={{0,4},{2,6},{4,0},{6,2},{16,20},{18,22},{20,16},{22,18},{32,36},{3... | collective-permute-start | bytes 786440 | tf_op jit(solution)/shard_map/ppermute | solution.py:51
  116.0 7.6 %collective-permute-start.20 = (bf16[4,256,128]{2,1,0:T(8,128)(2,1)S(1)}, bf16[4,256,128]{2,1,0:T(8,128)(2,1)S(1)}, u32[]{:S(2)}, u32[]{:S(2)}) collective-permute-start(bf16[4,256,128]{2,1,0:T(8,128)(2,1)S(1)} %get-tuple-element.18), channel_id=1, source_target_pairs={{0,6},{2,0},{4,2},{6,4},{16,22},{18,16},{20,18},{22,20},{32,38},{3... | collective-permute-start | bytes 786440 | tf_op jit(solution)/shard_map/ppermute | solution.py:51
  (11 other events, 67.4 us)
